TPU v7x, 256 devices: a whole 4x4x8 slice. The times are simulated.
256 devices in a mesh: row: 32 (over x, z), col: 8 (over y, core).
Axes of the slice: x: 4, y: 4, z: 8, core: 2. Of those that a mesh axis runs over, the one named last changes fastest.
Arguments:
- h_blocks: bfloat16 [4, 32, 16, 128, 128], P(None, 'row', 'col'), may hold values from -1.1953125 to 1.1953125
- p_blocks: bfloat16 [4, 32, 16, 128, 128], P(None, 'row', 'col'), may hold values from -1.1953125 to 1.1953125
- p1_blocks: bfloat16 [4, 32, 16, 128, 128], P(None, 'row', 'col'), may hold values from -1.1953125 to 1.1953125
- h_mask: int32 [4, 32, 16], P(None, 'row', 'col'), may hold values 0 or 1
- p_mask: int32 [4, 32, 16], P(None, 'row', 'col'), may hold values 0 or 1
- p1_mask: int32 [4, 32, 16], P(None, 'row', 'col'), may hold values 0 or 1
Outputs:
- commutator: bfloat16 [4, 32, 16, 128, 128], P(None, 'row', 'col')
- response: bfloat16 [4, 32, 16, 128, 128], P(None, 'row', 'col')
All inputs are finite; a program needn't handle non-finite values. No bound on the sum of `h_mask` or of `p_mask` or of `p1_mask` on one device may be relied on, other than what follows from the above.
Results may differ from a plain program's by a relative error of at most 0.001.
Values may be sent and summed in bfloat16 or wider, within the bound.
A program may use at most 128 MiB of HBM per device.

v0:
```python
import functools

import jax
import jax.numpy as jnp
from jax import lax
from jax.experimental import pallas as pl
from jax.experimental.pallas import tpu as pltpu
from jax.sharding import PartitionSpec as P

MESH = pl.DeviceIdType.MESH
NX, NY, NZ, NC = 4, 4, 8, 2
NM = 4
M, O = 0, 1
UP_HOPS = (4, 3)
DOWN_HOPS = (3, 4)


def kernel(own, out_m, out_o, strip, left, far, out_f, acc,
           z_recv, z_send, l_recv, y_send, c_send, f_send, p_recv, p_send, q_send,
           r_send, r_recv, local_sem):
    row, col = lax.axis_index("row"), lax.axis_index("col")
    x, z = row // NZ, row % NZ
    y, k = col // NC, col % NC
    u = col
    low = z <= u
    x_up, x_dn = (x + 1) % NX, (x + NX - 1) % NX
    z_up, z_dn = (z + 1) % NZ, (z + NZ - 1) % NZ
    y_up, y_dn = (y + 1) % NY, (y + NY - 1) % NY

    def dev(x_=x, y_=y, z_=z, k_=k):
        return (x_ * NZ + z_, y_ * NC + k_)

    dev_zu, dev_zd = dev(z_=z_up), dev(z_=z_dn)
    dev_yu, dev_yd = dev(y_=y_up), dev(y_=y_dn)
    dev_xu, dev_xd = dev(x_=x_up), dev(x_=x_dn)
    dev_c = dev(k_=1 - k)

    def remote(src, dst, send, recv, device):
        return pltpu.make_async_remote_copy(
            src_ref=src, dst_ref=dst, send_sem=send, recv_sem=recv,
            device_id=device, device_id_type=MESH)

    barrier = pltpu.get_barrier_semaphore()
    for peer in (dev_zu, dev_zd, dev_yu, dev_yd, dev_xu, dev_xd, dev_c):
        pl.semaphore_signal(barrier, inc=1, device_id=peer, device_id_type=MESH)
    pl.semaphore_wait(barrier, 7)

    def z_copy(up, hop, kind, m):
        origin = (z - hop + NZ) % NZ if up else (z + hop) % NZ
        src = own.at[M, m] if (hop == 0 and kind == M) else strip.at[origin, kind, m]
        return remote(src, strip.at[origin, kind, m], z_send.at[0 if up else 1, hop, kind, m],
                      z_recv.at[origin, kind, m], dev_zu if up else dev_zd)

    def z_arrival(up, hop, kind, m):
        origin = (z - hop + NZ) % NZ if up else (z + hop) % NZ
        return remote(strip.at[origin, kind, m], strip.at[origin, kind, m],
                      z_send.at[0 if up else 1, 0, kind, m], z_recv.at[origin, kind, m], dev_c)

    def z_round(hop, kind):
        for m in range(NM):
            for up in (True, False):
                limit = (UP_HOPS if up else DOWN_HOPS)[kind]
                if hop <= limit:
                    z_arrival(up, hop, kind, m).wait_recv()
                    if hop < limit:
                        z_copy(up, hop, kind, m).start()

    for m in range(NM):
        z_copy(True, 0, M, m).start()
        z_copy(False, 0, M, m).start()

    dev_f = (jnp.where(low, x_dn, x_up) * NZ + z, col)
    shift_up = jnp.where(x == NX - 1, 1, 0)
    shift_dn = jnp.where(x == 0, NM - 1, 0)
    f_shift = jnp.where(low, shift_dn, shift_up)

    def f_copy(m):
        there = (m + f_shift) % NM
        return remote(own.at[O, m], strip.at[z, O, there], f_send.at[m], z_recv.at[z, O, there], dev_f)

    for m in range(NM):
        f_copy(m).start()

    def l_wait(who, kind):
        remote(left.at[who, kind], left.at[who, kind], c_send.at[0, 0], l_recv.at[who, kind], dev_c).wait_recv()

    def y_copy(slot, up, kind, relay):
        if relay:
            who = (y_dn if up else y_up) * NC + k
            src = left.at[who, kind]
        else:
            who = u
            src = own.at[kind]
        return remote(src, left.at[who, kind], y_send.at[slot], l_recv.at[who, kind], dev_yu if up else dev_yd)

    y_copies = [y_copy(0, True, M, False), y_copy(1, False, O, False),
                y_copy(2, True, O, False), y_copy(3, False, M, False),
                y_copy(4, True, M, True), y_copy(5, False, O, True)]
    for c in y_copies[:4]:
        c.start()

    def c_copy(d, kind):
        who = ((y + d) % NY) * NC + k
        src = own.at[kind] if d == 0 else left.at[who, kind]
        return remote(src, left.at[who, kind], c_send.at[d, kind], l_recv.at[who, kind], dev_c)

    c_copy(0, M).start()
    c_copy(0, O).start()
    keep_left = pltpu.make_async_copy(own, left.at[u], local_sem.at[0])
    keep_left.start()
    keep_strip = pltpu.make_async_copy(own.at[M], strip.at[z, M], local_sem.at[1])
    keep_strip.start()

    need = (2 * y + 1 >= z, 2 * y < z)

    def far_wanted(side, who, kind):
        if side == 0:
            inside = who >= z if kind == O else who <= 2 * y + 1
        else:
            inside = who < z if kind == O else who > 2 * y
        return jnp.logical_and(need[side], inside)

    def far_sends(d, kind, act):
        who = ((y + d) % NY) * NC + k
        src = own.at[kind] if d == 0 else left.at[who, kind]
        for side in (0, 1):
            @pl.when(far_wanted(side, who, kind))
            def _():
                shift = shift_dn if side == 0 else shift_up
                for m in range(NM):
                    act(remote(src.at[m], far.at[side, who, kind, (m + shift) % NM],
                               p_send.at[side, d, kind, m], p_recv.at[side, who, kind],
                               dev_xd if side == 0 else dev_xu))

    def far_pass(d, kind):
        who = ((y + d) % NY) * NC + k
        for side in (0, 1):
            @pl.when(far_wanted(side, who, kind))
            def _():
                spot = far.at[side, who, kind]
                remote(spot, spot, q_send.at[side, d, kind], p_recv.at[side, who, kind], dev_c).wait_recv()
                remote(spot, spot, q_send.at[side, d, kind], p_recv.at[side, who, kind], dev_c).start()

    def start(c):
        c.start()

    side_f = jnp.where(low, 0, 1)
    far_sends(0, M, start)

    for m in range(NM):
        remote(strip.at[z, O, m], strip.at[z, O, m], f_send.at[m], z_recv.at[z, O, m], dev_c).wait_recv()
        z_copy(True, 0, O, m).start()
        z_copy(False, 0, O, m).start()
    f_keep = pltpu.make_async_copy(strip.at[z, O], far.at[side_f, u, O], local_sem.at[2])
    f_keep.start()
    f_pass = remote(strip.at[z, O], far.at[side_f, u, O], local_sem.at[3], p_recv.at[side_f, u, O], dev_c)
    f_pass.start()

    l_wait(y_dn * NC + k, M)
    y_copies[4].start()
    far_sends(3, M, start)
    c_copy(3, M).start()
    l_wait(y_up * NC + k, O)
    y_copies[5].start()
    far_sends(1, O, start)
    c_copy(1, O).start()

    z_round(1, M)

    l_wait(y_dn * NC + k, O)
    far_sends(3, O, start)
    c_copy(3, O).start()
    l_wait(y_up * NC + k, M)
    far_sends(1, M, start)
    c_copy(1, M).start()

    z_round(1, O)
    far_pass(0, M)
    z_round(2, M)

    who2 = ((y + 2) % NY) * NC + k
    l_wait(who2, M)
    far_sends(2, M, start)
    c_copy(2, M).start()
    l_wait(who2, O)
    far_sends(2, O, start)
    c_copy(2, O).start()

    z_round(2, O)
    far_pass(3, M)
    far_pass(1, O)
    z_round(3, M)
    far_pass(3, O)
    far_pass(1, M)
    z_round(3, O)
    z_round(4, M)
    z_round(4, O)
    far_pass(2, M)
    far_pass(2, O)

    keep_left.wait()
    keep_strip.wait()
    f_keep.wait()
    for d in range(NY):
        who = ((y + d) % NY) * NC + 1 - k
        for kind in (M, O):
            l_wait(who, kind)
            for side in (0, 1):
                @pl.when(far_wanted(side, who, kind))
                def _():
                    spot = far.at[side, who, kind]
                    remote(spot, spot, q_send.at[side, d, kind], p_recv.at[side, who, kind], dev_c).wait_recv()

    r_shift = jnp.where(low, shift_up, shift_dn)
    dev_r = (jnp.where(low, x_up, x_dn) * NZ + z, col)

    def r_copy(m):
        there = (m + r_shift) % NM
        return remote(out_f.at[m], out_o.at[there], r_send.at[m], r_recv.at[there], dev_r)

    def per_plane(m, _):
        def per_row(zp, _):
            same = (zp <= u) == low
            valid_own = jnp.where(zp > u, zp >= z, zp < z)
            valid_far = jnp.where(low, zp >= z, zp < z)
            zero = jnp.zeros((128, 128), jnp.bfloat16)

            def pick(ok, block):
                return jnp.where(ok, block, zero)

            def rhs(kind):
                h, p1, p = (strip[zp, kind, m, i] for i in range(3))
                return h, p1, p

            hm, am, pm = rhs(M)
            hf, af, pf = rhs(O)
            w_c = jnp.concatenate([am, -hm, af, -hf], axis=0)
            w_r = jnp.concatenate([am, pm, af, pf], axis=0)
            lm = [left[zp, M, m, i] for i in range(3)]
            lo = [pick(valid_own, left[zp, O, m, i]) for i in range(3)]
            fo = [pick(valid_far, far[side_f, zp, O, m, i]) for i in range(3)]
            fm = [pick(same, far[side_f, zp, M, m, i]) for i in range(3)]

            def lhs(i):
                top = jnp.concatenate([lm[i], lm[1], lo[i], lo[1]], axis=1)
                low_part = jnp.concatenate([fo[i], fo[1], fm[i], fm[1]], axis=1)
                return jnp.concatenate([top, low_part], axis=0)

            acc[0] += jnp.dot(lhs(0), w_c, preferred_element_type=jnp.float32)
            acc[1] += jnp.dot(lhs(2), w_r, preferred_element_type=jnp.float32)
            return 0

        acc[...] = jnp.zeros_like(acc)
        lax.fori_loop(0, NZ, per_row, 0)
        for i in range(2):
            out_f[m, i] = acc[i, 128:].astype(jnp.bfloat16)
            out_m[m, i] = acc[i, :128].astype(jnp.bfloat16)
        r_copy(m).start()
        return 0

    lax.fori_loop(0, NM, per_plane, 0)

    for m in range(NM):
        r_copy(m).wait_send()
        remote(out_o.at[m], out_o.at[m], r_send.at[m], r_recv.at[m], dev_c).wait_recv()
        f_copy(m).wait_send()
        for kind in (M, O):
            for up in (True, False):
                for hop in range((UP_HOPS if up else DOWN_HOPS)[kind]):
                    z_copy(up, hop, kind, m).wait_send()
    for c in y_copies:
        c.wait_send()
    f_pass.wait_send()
    for d in range(NY):
        who = ((y + d) % NY) * NC + k
        for kind in (M, O):
            c_copy(d, kind).wait_send()
            if (d, kind) != (0, O):
                far_sends(d, kind, lambda c: c.wait_send())
                for side in (0, 1):
                    @pl.when(far_wanted(side, who, kind))
                    def _():
                        spot = far.at[side, who, kind]
                        remote(spot, spot, q_send.at[side, d, kind], p_recv.at[side, who, kind], dev_c).wait_send()


def exchange(own):
    dma = pltpu.SemaphoreType.DMA
    block = (128, 128)
    return pl.pallas_call(
        kernel,
        out_shape=(jax.ShapeDtypeStruct((NM, 2) + block, jnp.bfloat16),) * 2,
        in_specs=[pl.BlockSpec(memory_space=pltpu.VMEM)],
        out_specs=(pl.BlockSpec(memory_space=pltpu.VMEM),) * 2,
        scratch_shapes=[
            pltpu.VMEM((NZ, 2, NM, 3) + block, jnp.bfloat16),
            pltpu.VMEM((8, 2, NM, 3) + block, jnp.bfloat16),
            pltpu.VMEM((2, 8, 2, NM, 3) + block, jnp.bfloat16),
            pltpu.VMEM((NM, 2) + block, jnp.bfloat16),
            pltpu.VMEM((2, 256, 128), jnp.float32),
            dma((NZ, 2, NM)),
            dma((2, 4, 2, NM)),
            dma((8, 2)),
            dma((6,)),
            dma((NY, 2)),
            dma((NM,)),
            dma((2, 8, 2)),
            dma((2, NY, 2, NM)),
            dma((2, NY, 2)),
            dma((NM,)),
            dma((NM,)),
            dma((4,)),
        ],
        compiler_params=pltpu.CompilerParams(collective_id=0, has_side_effects=True),
        name="exchange",
    )(own)


def per_device(h_blocks, p_blocks, p1_blocks, h_mask, p_mask, p1_mask):
    row, col = lax.axis_index("row"), lax.axis_index("col")
    low = (row % NZ) <= col

    def masked(values, pattern):
        return values[:, 0] * pattern[:, 0][:, :, None, None].astype(values.dtype)

    blocks = jnp.stack((masked(h_blocks, h_mask), masked(p1_blocks, p1_mask), masked(p_blocks, p_mask)), axis=1)
    first, second = blocks[:, :, 0], blocks[:, :, 1]
    own = jnp.stack((jnp.where(low, second, first), jnp.where(low, first, second)))
    out_m, out_o = exchange(own)
    pattern = p1_mask[:, 0][:, :, None, None].astype(jnp.bfloat16)

    def placed(i):
        m, o = out_m[:, i], out_o[:, i]
        return (jnp.stack((jnp.where(low, o, m), jnp.where(low, m, o)), axis=1) * pattern)[:, None]

    return placed(0), placed(1)


def solution(mesh):
    blocks = P(None, "row", "col", None, None)
    masks = P(None, "row", "col")
    return jax.shard_map(
        per_device, mesh=mesh, in_specs=(blocks,) * 3 + (masks,) * 3,
        out_specs=(blocks, blocks), check_vma=False,
    )
```

profile of v0, /device:TPU:25, one launch (start us, length us, event | category | flops | bytes accessed | tf_op | source)
XLA Modules:
  0.0 102.2 jit_solution(11293301281103759459)
XLA Ops:
  0.6 0.0 copy-start.2
  0.7 0.7 copy-done.2
  1.3 0.0 copy-start.3
  1.3 0.7 copy-done.3
  2.0 0.0 copy-start.4
  2.0 0.7 copy-done.4
  2.7 0.0 copy-start
  2.7 0.0 copy-start.1
  2.7 1.1 %copy_multiply_fusion.2 = bf16[4,1,2,128,128]{4,3,1,0,2:T(8,128)(2,1)S(1)} fusion(bf16[4,1,2,128,128]{4,3,2,1,0:T(8,128)(2,1)} %param.6, bf16[4,2]{0,1:T(2,128)(2,1)S(1)} %convert_bitcast_fusion.2), kind=kLoop, calls=%fused_computation.8 | loop fusion | flops 131072 | bytes 524304 | tf_op jit(solution)/shard_map/mul | solution.py:324
  3.8 0.0 copy-done
  3.8 0.0 copy-done.1
  3.8 0.1 copy_multiply_fusion
  3.9 0.1 pad_maximum_fusion
  4.0 0.1 select_bitcast_fusion.1
  4.1 1.0 pad_maximum_fusion.1.own
  5.0 94.3 %exchange.1 = (bf16[4,2,128,128]{3,2,1,0:T(8,128)(2,1)}, bf16[4,2,128,128]{3,2,1,0:T(8,128)(2,1)}) custom-call(bf16[2,4,3,128,128]{4,3,2,1,0:T(8,128)(2,1)} %pad_maximum_fusion.1.own), custom_call_target="tpu_custom_call" | custom-call | tf_op jit(solution)/shard_map/exchange/pallas_call | solution.py:290
  99.3 1.2 %select_bitcast_fusion.3 = (bf16[4,1,1,128,128]{4,3,1,0,2:T(8,128)(2,1)S(1)}, bf16[4,1,1,128,128]{4,3,0,2,1:T(8,128)(2,1)S(1)}, bf16[4,1,1,128,128]{4,3,1,0,2:T(8,128)(2,1)S(1)}, bf16[4,1,1,128,128]{4,3,0,2,1:T(8,128)(2,1)S(1)}) fusion(pred[]{:T(512)S(6)} %le.3, bf16[4,2,128,128]{3,2,1,0:T(8,128)(2,1)} %get-tuple-element.4, ...), kind=kLoop, calls=%fused_computation.10 | loop fusion | flops 262144 | bytes 1048577 | tf_op jit(solution)/shard_map/stack | solution.py:334
  100.6 0.1 maximum_multiply_fusion.1
  100.7 0.1 maximum_multiply_fusion
  100.8 0.7 copy.17
  101.5 0.7 copy.18
  (3 shorter events, 0.0 us)
Async XLA Ops:
  0.6 0.7 copy-start.2
  1.3 0.7 copy-start.3
  2.0 0.7 copy-start.4
  2.7 1.1 %copy-start = (bf16[4,1,2,128,128]{4,3,2,1,0:T(8,128)(2,1)S(1)}, bf16[4,1,2,128,128]{4,3,2,1,0:T(8,128)(2,1)}, u32[]{:S(2)}) copy-start(bf16[4,1,2,128,128]{4,3,2,1,0:T(8,128)(2,1)} %param.7) | copy-start | bytes 786436
  2.7 1.1 %copy-start.1 = (bf16[4,1,2,128,128]{4,3,2,1,0:T(8,128)(2,1)S(1)}, bf16[4,1,2,128,128]{4,3,2,1,0:T(8,128)(2,1)}, u32[]{:S(2)}) copy-start(bf16[4,1,2,128,128]{4,3,2,1,0:T(8,128)(2,1)} %param.8) | copy-start | bytes 786436
where the time goes:
time: 102 us
  Pallas kernels  94.3 us (92%)
  other arithmetic  3.71 us (4%)
  local copies, waits for them, and re-layouts  3.47 us (3%)
    pallas_call x1, Pallas kernels, exchange(): pl.pallas_call(kernel, out_shape=(jax.ShapeDtypeStruct((NM, 2) + block, j...  94.3 us
    unnamed x12, local copies, waits for them, and re-layouts  3.47 us

commit v1 on v0

--- a/solution.py
+++ b/solution.py
@@ -17,7 +17,7 @@
 
 def kernel(own, out_m, out_o, strip, left, far, out_f, acc,
            z_recv, z_send, l_recv, y_send, c_send, f_send, p_recv, p_send, q_send,
-           r_send, r_recv, local_sem):
+           fy_send, r_send, r_recv, local_sem):
     row, col = lax.axis_index("row"), lax.axis_index("col")
     x, z = row // NZ, row % NZ
     y, k = col // NC, col % NC
@@ -111,20 +111,26 @@
     keep_strip = pltpu.make_async_copy(own.at[M], strip.at[z, M], local_sem.at[1])
     keep_strip.start()
 
-    need = (2 * y + 1 >= z, 2 * y < z)
-
-    def far_wanted(side, who, kind):
+    def far_wanted(side, who, kind, at):
         if side == 0:
-            inside = who >= z if kind == O else who <= 2 * y + 1
-        else:
-            inside = who < z if kind == O else who > 2 * y
-        return jnp.logical_and(need[side], inside)
+            inside = who >= z if kind == O else who <= 2 * at + 1
+            return jnp.logical_and(2 * at + 1 >= z, inside)
+        inside = who < z if kind == O else who > 2 * at
+        return jnp.logical_and(2 * at < z, inside)
+
+    def far_by_x(side, d, kind):
+        home = (y + d) % NY
+        who = home * NC + k
+        wanted = far_wanted(side, who, kind, y)
+        if d in (1, 3):
+            wanted = jnp.logical_and(wanted, jnp.logical_not(far_wanted(side, who, kind, home)))
+        return wanted
 
     def far_sends(d, kind, act):
         who = ((y + d) % NY) * NC + k
         src = own.at[kind] if d == 0 else left.at[who, kind]
         for side in (0, 1):
-            @pl.when(far_wanted(side, who, kind))
+            @pl.when(far_by_x(side, d, kind))
             def _():
                 shift = shift_dn if side == 0 else shift_up
                 for m in range(NM):
@@ -132,10 +138,19 @@
                                p_send.at[side, d, kind, m], p_recv.at[side, who, kind],
                                dev_xd if side == 0 else dev_xu))
 
+    def far_y(kind, act):
+        for side in (0, 1):
+            for way, (there, device) in enumerate(((y_up, dev_yu), (y_dn, dev_yd))):
+                @pl.when(jnp.logical_and(far_wanted(side, u, kind, y), far_wanted(side, u, kind, there)))
+                def _():
+                    src = strip.at[z, O] if kind == O else far.at[side, u, M]
+                    act(remote(src, far.at[side, u, kind], fy_send.at[side, way, kind],
+                               p_recv.at[side, u, kind], device))
+
     def far_pass(d, kind):
         who = ((y + d) % NY) * NC + k
         for side in (0, 1):
-            @pl.when(far_wanted(side, who, kind))
+            @pl.when(far_wanted(side, who, kind, y))
             def _():
                 spot = far.at[side, who, kind]
                 remote(spot, spot, q_send.at[side, d, kind], p_recv.at[side, who, kind], dev_c).wait_recv()
@@ -164,6 +179,7 @@
     y_copies[5].start()
     far_sends(1, O, start)
     c_copy(1, O).start()
+    far_y(O, start)
 
     z_round(1, M)
 
@@ -174,8 +190,9 @@
     far_sends(1, M, start)
     c_copy(1, M).start()
 
+    far_pass(0, M)
+    far_y(M, start)
     z_round(1, O)
-    far_pass(0, M)
     z_round(2, M)
 
     who2 = ((y + 2) % NY) * NC + k
@@ -187,15 +204,13 @@
     c_copy(2, O).start()
 
     z_round(2, O)
-    far_pass(3, M)
+    far_pass(3, O)
     far_pass(1, O)
     z_round(3, M)
-    far_pass(3, O)
+    far_pass(3, M)
     far_pass(1, M)
+    far_pass(2, M)
     z_round(3, O)
-    z_round(4, M)
-    z_round(4, O)
-    far_pass(2, M)
     far_pass(2, O)
 
     keep_left.wait()
@@ -206,7 +221,7 @@
         for kind in (M, O):
             l_wait(who, kind)
             for side in (0, 1):
-                @pl.when(far_wanted(side, who, kind))
+                @pl.when(far_wanted(side, who, kind, y))
                 def _():
                     spot = far.at[side, who, kind]
                     remote(spot, spot, q_send.at[side, d, kind], p_recv.at[side, who, kind], dev_c).wait_recv()
@@ -218,47 +233,57 @@
         there = (m + r_shift) % NM
         return remote(out_f.at[m], out_o.at[there], r_send.at[m], r_recv.at[there], dev_r)
 
-    def per_plane(m, _):
-        def per_row(zp, _):
-            same = (zp <= u) == low
-            valid_own = jnp.where(zp > u, zp >= z, zp < z)
-            valid_far = jnp.where(low, zp >= z, zp < z)
-            zero = jnp.zeros((128, 128), jnp.bfloat16)
-
-            def pick(ok, block):
-                return jnp.where(ok, block, zero)
-
-            def rhs(kind):
-                h, p1, p = (strip[zp, kind, m, i] for i in range(3))
-                return h, p1, p
-
-            hm, am, pm = rhs(M)
-            hf, af, pf = rhs(O)
-            w_c = jnp.concatenate([am, -hm, af, -hf], axis=0)
-            w_r = jnp.concatenate([am, pm, af, pf], axis=0)
-            lm = [left[zp, M, m, i] for i in range(3)]
-            lo = [pick(valid_own, left[zp, O, m, i]) for i in range(3)]
-            fo = [pick(valid_far, far[side_f, zp, O, m, i]) for i in range(3)]
-            fm = [pick(same, far[side_f, zp, M, m, i]) for i in range(3)]
-
-            def lhs(i):
-                top = jnp.concatenate([lm[i], lm[1], lo[i], lo[1]], axis=1)
-                low_part = jnp.concatenate([fo[i], fo[1], fm[i], fm[1]], axis=1)
-                return jnp.concatenate([top, low_part], axis=0)
-
-            acc[0] += jnp.dot(lhs(0), w_c, preferred_element_type=jnp.float32)
-            acc[1] += jnp.dot(lhs(2), w_r, preferred_element_type=jnp.float32)
-            return 0
-
-        acc[...] = jnp.zeros_like(acc)
-        lax.fori_loop(0, NZ, per_row, 0)
-        for i in range(2):
-            out_f[m, i] = acc[i, 128:].astype(jnp.bfloat16)
-            out_m[m, i] = acc[i, :128].astype(jnp.bfloat16)
+    zero = jnp.zeros((128, 128), jnp.bfloat16)
+
+    def pick(ok, block):
+        return jnp.where(ok, block, zero)
+
+    def products(m, zp):
+        same = (zp <= u) == low
+        valid_own = jnp.where(zp > u, zp >= z, zp < z)
+        valid_far = jnp.where(low, zp >= z, zp < z)
+        hm, am, pm = (strip[zp, M, m, i] for i in range(3))
+        hf, af, pf = (strip[zp, O, m, i] for i in range(3))
+        w_c = jnp.concatenate([am, -hm, af, -hf], axis=0)
+        w_r = jnp.concatenate([am, pm, af, pf], axis=0)
+        lm = [left[zp, M, m, i] for i in range(3)]
+        lo = [pick(valid_own, left[zp, O, m, i]) for i in range(3)]
+        fo = [pick(valid_far, far[side_f, zp, O, m, i]) for i in range(3)]
+        fm = [pick(same, far[side_f, zp, M, m, i]) for i in range(3)]
+
+        def lhs(i):
+            top = jnp.concatenate([lm[i], lm[1], lo[i], lo[1]], axis=1)
+            low_part = jnp.concatenate([fo[i], fo[1], fm[i], fm[1]], axis=1)
+            return jnp.concatenate([top, low_part], axis=0)
+
+        return (jnp.dot(lhs(0), w_c, preferred_element_type=jnp.float32),
+                jnp.dot(lhs(2), w_r, preferred_element_type=jnp.float32))
+
+    def add(m, zp):
+        c, r = products(m, zp)
+        acc[m, 0] += c
+        acc[m, 1] += r
+
+    for m in range(NM):
+        acc[m] = jnp.zeros((2, 256, 128), jnp.float32)
+
+    def early(i, _):
+        d = i % (NZ - 1)
+        add(i // (NZ - 1), (z + jnp.where(d > 3, d + 1, d)) % NZ)
+        return 0
+
+    lax.fori_loop(0, NM * (NZ - 1), early, 0)
+
+    for m in range(NM):
+        z_arrival(True, 4, M, m).wait_recv()
+        z_arrival(False, 4, O, m).wait_recv()
+        c, r = products(m, (z + 4) % NZ)
+        c, r = c + acc[m, 0], r + acc[m, 1]
+        out_f[m, 0] = c[128:].astype(jnp.bfloat16)
+        out_f[m, 1] = r[128:].astype(jnp.bfloat16)
+        out_m[m, 0] = c[:128].astype(jnp.bfloat16)
+        out_m[m, 1] = r[:128].astype(jnp.bfloat16)
         r_copy(m).start()
-        return 0
-
-    lax.fori_loop(0, NM, per_plane, 0)
 
     for m in range(NM):
         r_copy(m).wait_send()
@@ -271,6 +296,8 @@
     for c in y_copies:
         c.wait_send()
     f_pass.wait_send()
+    far_y(M, lambda c: c.wait_send())
+    far_y(O, lambda c: c.wait_send())
     for d in range(NY):
         who = ((y + d) % NY) * NC + k
         for kind in (M, O):
@@ -278,7 +305,7 @@
             if (d, kind) != (0, O):
                 far_sends(d, kind, lambda c: c.wait_send())
                 for side in (0, 1):
-                    @pl.when(far_wanted(side, who, kind))
+                    @pl.when(far_wanted(side, who, kind, y))
                     def _():
                         spot = far.at[side, who, kind]
                         remote(spot, spot, q_send.at[side, d, kind], p_recv.at[side, who, kind], dev_c).wait_send()
@@ -297,7 +324,7 @@
             pltpu.VMEM((8, 2, NM, 3) + block, jnp.bfloat16),
             pltpu.VMEM((2, 8, 2, NM, 3) + block, jnp.bfloat16),
             pltpu.VMEM((NM, 2) + block, jnp.bfloat16),
-            pltpu.VMEM((2, 256, 128), jnp.float32),
+            pltpu.VMEM((NM, 2, 256, 128), jnp.float32),
             dma((NZ, 2, NM)),
             dma((2, 4, 2, NM)),
             dma((8, 2)),
@@ -307,6 +334,7 @@
             dma((2, 8, 2)),
             dma((2, NY, 2, NM)),
             dma((2, NY, 2)),
+            dma((2, 2, 2)),
             dma((NM,)),
             dma((NM,)),
             dma((4,)),

time: 102 us -> 94.9 us (0.930)
  the two profiles are of different devices: /device:TPU:25 before, /device:TPU:1 now
where the time goes in v1:
time: 94.9 us; the launch traced here: 94.7 us
  Pallas kernels  86.8 us (91%)
  other arithmetic  3.71 us (4%)
  local copies, waits for them, and re-layouts  3.47 us (4%)
    pallas_call x1, Pallas kernels, exchange(): pl.pallas_call(kernel, out_shape=(jax.ShapeDtypeStruct((NM, 2) + block, j...  86.8 us
    unnamed x12, local copies, waits for them, and re-layouts  3.47 us

profile of v1, /device:TPU:1, one launch (start us, length us, event | category | flops | bytes accessed | tf_op | source)
XLA Modules:
  0.0 94.7 jit_solution(6267881083537258803)
XLA Ops:
  0.6 0.0 copy-start.2
  0.7 0.7 copy-done.2
  1.3 0.0 copy-start.3
  1.3 0.7 copy-done.3
  2.0 0.0 copy-start.4
  2.0 0.7 copy-done.4
  2.7 0.0 copy-start
  2.7 0.0 copy-start.1
  2.7 1.1 %copy_multiply_fusion.2 = bf16[4,1,2,128,128]{4,3,1,0,2:T(8,128)(2,1)S(1)} fusion(bf16[4,1,2,128,128]{4,3,2,1,0:T(8,128)(2,1)} %param.6, bf16[4,2]{0,1:T(2,128)(2,1)S(1)} %convert_bitcast_fusion.2), kind=kLoop, calls=%fused_computation.8 | loop fusion | flops 131072 | bytes 524304 | tf_op jit(solution)/shard_map/mul | solution.py:352
  3.8 0.0 copy-done
  3.8 0.0 copy-done.1
  3.8 0.1 copy_multiply_fusion
  3.9 0.1 pad_maximum_fusion
  4.0 0.1 select_bitcast_fusion.1
  4.1 1.0 %pad_maximum_fusion.1.own = bf16[2,4,3,128,128]{4,3,2,1,0:T(8,128)(2,1)} fusion(bf16[1,4,3,128,128]{4,3,2,1,0:T(8,128)(2,1)S(1)} %get-tuple-element.9, bf16[1,4,3,128,128]{4,3,2,1,0:T(8,128)(2,1)S(1)} %get-tuple-element.8), kind=kLoop, calls=%fused_computation.1 | loop fusion | flops 393216 | bytes 1572864 | tf_op jit(solution)/shard_map/stack | solution.py:356
  5.0 86.8 %exchange.1 = (bf16[4,2,128,128]{3,2,1,0:T(8,128)(2,1)}, bf16[4,2,128,128]{3,2,1,0:T(8,128)(2,1)}) custom-call(bf16[2,4,3,128,128]{4,3,2,1,0:T(8,128)(2,1)} %pad_maximum_fusion.1.own), custom_call_target="tpu_custom_call" | custom-call | tf_op jit(solution)/shard_map/exchange/pallas_call | solution.py:317
  91.8 1.2 %select_bitcast_fusion.3 = (bf16[4,1,1,128,128]{4,3,1,0,2:T(8,128)(2,1)S(1)}, bf16[4,1,1,128,128]{4,3,0,2,1:T(8,128)(2,1)S(1)}, bf16[4,1,1,128,128]{4,3,1,0,2:T(8,128)(2,1)S(1)}, bf16[4,1,1,128,128]{4,3,0,2,1:T(8,128)(2,1)S(1)}) fusion(pred[]{:T(512)S(6)} %le.3, bf16[4,2,128,128]{3,2,1,0:T(8,128)(2,1)} %get-tuple-element.4, ...), kind=kLoop, calls=%fused_computation.10 | loop fusion | flops 262144 | bytes 1048577 | tf_op jit(solution)/shard_map/stack | solution.py:362
  93.1 0.1 maximum_multiply_fusion.1
  93.2 0.1 maximum_multiply_fusion
  93.2 0.7 copy.17
  94.0 0.7 copy.18
  (3 shorter events, 0.0 us)
Async XLA Ops:
  0.6 0.7 copy-start.2
  1.3 0.7 copy-start.3
  2.0 0.7 copy-start.4
  2.7 1.1 %copy-start = (bf16[4,1,2,128,128]{4,3,2,1,0:T(8,128)(2,1)S(1)}, bf16[4,1,2,128,128]{4,3,2,1,0:T(8,128)(2,1)}, u32[]{:S(2)}) copy-start(bf16[4,1,2,128,128]{4,3,2,1,0:T(8,128)(2,1)} %param.7) | copy-start | bytes 786436
  2.7 1.1 %copy-start.1 = (bf16[4,1,2,128,128]{4,3,2,1,0:T(8,128)(2,1)S(1)}, bf16[4,1,2,128,128]{4,3,2,1,0:T(8,128)(2,1)}, u32[]{:S(2)}) copy-start(bf16[4,1,2,128,128]{4,3,2,1,0:T(8,128)(2,1)} %param.8) | copy-start | bytes 786436

commit v2 on v1

--- a/solution.py
+++ b/solution.py
@@ -15,7 +15,7 @@
 DOWN_HOPS = (3, 4)
 
 
-def kernel(own, out_m, out_o, strip, left, far, out_f, acc,
+def kernel(h_ref, p1_ref, p_ref, h_mask, p1_mask, p_mask, out_c, out_r, raw, strip, left, far, out_f, back, acc,
            z_recv, z_send, l_recv, y_send, c_send, f_send, p_recv, p_send, q_send,
            fy_send, r_send, r_recv, local_sem):
     row, col = lax.axis_index("row"), lax.axis_index("col")
@@ -43,12 +43,29 @@
     barrier = pltpu.get_barrier_semaphore()
     for peer in (dev_zu, dev_zd, dev_yu, dev_yd, dev_xu, dev_xd, dev_c):
         pl.semaphore_signal(barrier, inc=1, device_id=peer, device_id_type=MESH)
+
+    slot_m = jnp.where(low, 1, 0)
+    slots = (slot_m, 1 - slot_m)
+    loads = [pltpu.make_async_copy(ref, raw.at[i], local_sem.at[i]) for i, ref in enumerate((h_ref, p1_ref, p_ref))]
+    for c in loads:
+        c.start()
+    for m in range(NM):
+        acc[m] = jnp.zeros((2, 2, 128, 128), jnp.float32)
+    for i, (c, mask) in enumerate(zip(loads, (h_mask, p1_mask, p_mask))):
+        c.wait()
+        for kind in (M, O):
+            for m in range(NM):
+                keep = mask[slots[kind], m].astype(jnp.float32)
+                block = (raw[i, m, slots[kind]].astype(jnp.float32) * keep).astype(jnp.bfloat16)
+                left[u, kind, m, i] = block
+                if kind == M:
+                    strip[z, M, m, i] = block
+    own = left.at[u]
     pl.semaphore_wait(barrier, 7)
 
     def z_copy(up, hop, kind, m):
         origin = (z - hop + NZ) % NZ if up else (z + hop) % NZ
-        src = own.at[M, m] if (hop == 0 and kind == M) else strip.at[origin, kind, m]
-        return remote(src, strip.at[origin, kind, m], z_send.at[0 if up else 1, hop, kind, m],
+        return remote(strip.at[origin, kind, m], strip.at[origin, kind, m], z_send.at[0 if up else 1, hop, kind, m],
                       z_recv.at[origin, kind, m], dev_zu if up else dev_zd)
 
     def z_arrival(up, hop, kind, m):
@@ -106,10 +123,6 @@
 
     c_copy(0, M).start()
     c_copy(0, O).start()
-    keep_left = pltpu.make_async_copy(own, left.at[u], local_sem.at[0])
-    keep_left.start()
-    keep_strip = pltpu.make_async_copy(own.at[M], strip.at[z, M], local_sem.at[1])
-    keep_strip.start()
 
     def far_wanted(side, who, kind, at):
         if side == 0:
@@ -166,9 +179,9 @@
         remote(strip.at[z, O, m], strip.at[z, O, m], f_send.at[m], z_recv.at[z, O, m], dev_c).wait_recv()
         z_copy(True, 0, O, m).start()
         z_copy(False, 0, O, m).start()
-    f_keep = pltpu.make_async_copy(strip.at[z, O], far.at[side_f, u, O], local_sem.at[2])
+    f_keep = pltpu.make_async_copy(strip.at[z, O], far.at[side_f, u, O], local_sem.at[3])
     f_keep.start()
-    f_pass = remote(strip.at[z, O], far.at[side_f, u, O], local_sem.at[3], p_recv.at[side_f, u, O], dev_c)
+    f_pass = remote(strip.at[z, O], far.at[side_f, u, O], local_sem.at[4], p_recv.at[side_f, u, O], dev_c)
     f_pass.start()
 
     l_wait(y_dn * NC + k, M)
@@ -206,6 +219,43 @@
     z_round(2, O)
     far_pass(3, O)
     far_pass(1, O)
+
+    zero = jnp.zeros((128, 128), jnp.bfloat16)
+
+    def products(r, m, zp):
+        hm, am, pm = (strip[zp, M, m, i] for i in range(3))
+        hf, af, pf = (strip[zp, O, m, i] for i in range(3))
+        if r == 0:
+            ok = jnp.where(zp > u, zp >= z, zp < z)
+            first = [left[zp, M, m, i] for i in range(3)]
+            second = [jnp.where(ok, left[zp, O, m, i], zero) for i in range(3)]
+        else:
+            ok_m = jnp.where(low, zp >= z, zp < z)
+            ok_f = (zp <= u) == low
+            first = [jnp.where(ok_m, far[side_f, zp, O, m, i], zero) for i in range(3)]
+            second = [jnp.where(ok_f, far[side_f, zp, M, m, i], zero) for i in range(3)]
+        lh, la, lp = (jnp.concatenate([f, s], axis=1) for f, s in zip(first, second))
+        one = jnp.dot(jnp.concatenate([lh, lp], axis=0), jnp.concatenate([am, af], axis=0),
+                      preferred_element_type=jnp.float32)
+        rhs = jnp.concatenate([jnp.concatenate([-hm, pm], axis=1), jnp.concatenate([-hf, pf], axis=1)], axis=0)
+        two = jnp.dot(la, rhs, preferred_element_type=jnp.float32)
+        return one[:128] + two[:, :128], one[128:] + two[:, 128:]
+
+    def add(r, m, zp):
+        c, s = products(r, m, zp)
+        acc[m, r, 0] += c
+        acc[m, r, 1] += s
+
+    for d in range(NY):
+        for kind in (M, O):
+            l_wait(((y + d) % NY) * NC + 1 - k, kind)
+
+    def near(i, _):
+        add(0, i // 5, (z + i % 5 + 6) % NZ)
+        return 0
+
+    lax.fori_loop(0, NM * 5, near, 0)
+
     z_round(3, M)
     far_pass(3, M)
     far_pass(1, M)
@@ -213,13 +263,16 @@
     z_round(3, O)
     far_pass(2, O)
 
-    keep_left.wait()
-    keep_strip.wait()
+    def third(i, _):
+        add(0, i // 2, (z + 3 + 2 * (i % 2)) % NZ)
+        return 0
+
+    lax.fori_loop(0, NM * 2, third, 0)
+
     f_keep.wait()
     for d in range(NY):
         who = ((y + d) % NY) * NC + 1 - k
         for kind in (M, O):
-            l_wait(who, kind)
             for side in (0, 1):
                 @pl.when(far_wanted(side, who, kind, y))
                 def _():
@@ -231,63 +284,34 @@
 
     def r_copy(m):
         there = (m + r_shift) % NM
-        return remote(out_f.at[m], out_o.at[there], r_send.at[m], r_recv.at[there], dev_r)
-
-    zero = jnp.zeros((128, 128), jnp.bfloat16)
-
-    def pick(ok, block):
-        return jnp.where(ok, block, zero)
-
-    def products(m, zp):
-        same = (zp <= u) == low
-        valid_own = jnp.where(zp > u, zp >= z, zp < z)
-        valid_far = jnp.where(low, zp >= z, zp < z)
-        hm, am, pm = (strip[zp, M, m, i] for i in range(3))
-        hf, af, pf = (strip[zp, O, m, i] for i in range(3))
-        w_c = jnp.concatenate([am, -hm, af, -hf], axis=0)
-        w_r = jnp.concatenate([am, pm, af, pf], axis=0)
-        lm = [left[zp, M, m, i] for i in range(3)]
-        lo = [pick(valid_own, left[zp, O, m, i]) for i in range(3)]
-        fo = [pick(valid_far, far[side_f, zp, O, m, i]) for i in range(3)]
-        fm = [pick(same, far[side_f, zp, M, m, i]) for i in range(3)]
-
-        def lhs(i):
-            top = jnp.concatenate([lm[i], lm[1], lo[i], lo[1]], axis=1)
-            low_part = jnp.concatenate([fo[i], fo[1], fm[i], fm[1]], axis=1)
-            return jnp.concatenate([top, low_part], axis=0)
-
-        return (jnp.dot(lhs(0), w_c, preferred_element_type=jnp.float32),
-                jnp.dot(lhs(2), w_r, preferred_element_type=jnp.float32))
-
-    def add(m, zp):
-        c, r = products(m, zp)
-        acc[m, 0] += c
-        acc[m, 1] += r
-
-    for m in range(NM):
-        acc[m] = jnp.zeros((2, 256, 128), jnp.float32)
-
-    def early(i, _):
-        d = i % (NZ - 1)
-        add(i // (NZ - 1), (z + jnp.where(d > 3, d + 1, d)) % NZ)
-        return 0
-
-    lax.fori_loop(0, NM * (NZ - 1), early, 0)
-
-    for m in range(NM):
+        return remote(out_f.at[m], back.at[there], r_send.at[m], r_recv.at[there], dev_r)
+
+    def put(m, kind, c, s):
+        keep = p1_mask[slots[kind], m].astype(jnp.float32)
+        out_c[m, slots[kind]] = (c * keep).astype(jnp.bfloat16)
+        out_r[m, slots[kind]] = (s * keep).astype(jnp.bfloat16)
+
+    for m in range(NM):
+        def early(i, _):
+            add(1, m, (z + i + 5) % NZ)
+            return 0
+
+        lax.fori_loop(0, NZ - 1, early, 0)
         z_arrival(True, 4, M, m).wait_recv()
         z_arrival(False, 4, O, m).wait_recv()
-        c, r = products(m, (z + 4) % NZ)
-        c, r = c + acc[m, 0], r + acc[m, 1]
-        out_f[m, 0] = c[128:].astype(jnp.bfloat16)
-        out_f[m, 1] = r[128:].astype(jnp.bfloat16)
-        out_m[m, 0] = c[:128].astype(jnp.bfloat16)
-        out_m[m, 1] = r[:128].astype(jnp.bfloat16)
+        c, s = products(1, m, (z + 4) % NZ)
+        out_f[m, 0] = (c + acc[m, 1, 0]).astype(jnp.bfloat16)
+        out_f[m, 1] = (s + acc[m, 1, 1]).astype(jnp.bfloat16)
+        c, s = products(0, m, (z + 4) % NZ)
+        put(m, M, c + acc[m, 0, 0], s + acc[m, 0, 1])
         r_copy(m).start()
 
     for m in range(NM):
+        remote(back.at[m], back.at[m], r_send.at[m], r_recv.at[m], dev_c).wait_recv()
+        put(m, O, back[m, 0].astype(jnp.float32), back[m, 1].astype(jnp.float32))
+
+    for m in range(NM):
         r_copy(m).wait_send()
-        remote(out_o.at[m], out_o.at[m], r_send.at[m], r_recv.at[m], dev_c).wait_recv()
         f_copy(m).wait_send()
         for kind in (M, O):
             for up in (True, False):
@@ -311,20 +335,22 @@
                         remote(spot, spot, q_send.at[side, d, kind], p_recv.at[side, who, kind], dev_c).wait_send()
 
 
-def exchange(own):
+def exchange(values, masks):
     dma = pltpu.SemaphoreType.DMA
     block = (128, 128)
     return pl.pallas_call(
         kernel,
         out_shape=(jax.ShapeDtypeStruct((NM, 2) + block, jnp.bfloat16),) * 2,
-        in_specs=[pl.BlockSpec(memory_space=pltpu.VMEM)],
+        in_specs=[pl.BlockSpec(memory_space=pl.ANY)] * 3 + [pl.BlockSpec(memory_space=pltpu.SMEM)] * 3,
         out_specs=(pl.BlockSpec(memory_space=pltpu.VMEM),) * 2,
         scratch_shapes=[
+            pltpu.VMEM((3, NM, 2) + block, jnp.bfloat16),
             pltpu.VMEM((NZ, 2, NM, 3) + block, jnp.bfloat16),
             pltpu.VMEM((8, 2, NM, 3) + block, jnp.bfloat16),
             pltpu.VMEM((2, 8, 2, NM, 3) + block, jnp.bfloat16),
             pltpu.VMEM((NM, 2) + block, jnp.bfloat16),
-            pltpu.VMEM((NM, 2, 256, 128), jnp.float32),
+            pltpu.VMEM((NM, 2) + block, jnp.bfloat16),
+            pltpu.VMEM((NM, 2, 2) + block, jnp.float32),
             dma((NZ, 2, NM)),
             dma((2, 4, 2, NM)),
             dma((8, 2)),
@@ -337,31 +363,17 @@
             dma((2, 2, 2)),
             dma((NM,)),
             dma((NM,)),
-            dma((4,)),
+            dma((5,)),
         ],
         compiler_params=pltpu.CompilerParams(collective_id=0, has_side_effects=True),
         name="exchange",
-    )(own)
+    )(*values, *masks)
 
 
 def per_device(h_blocks, p_blocks, p1_blocks, h_mask, p_mask, p1_mask):
-    row, col = lax.axis_index("row"), lax.axis_index("col")
-    low = (row % NZ) <= col
-
-    def masked(values, pattern):
-        return values[:, 0] * pattern[:, 0][:, :, None, None].astype(values.dtype)
-
-    blocks = jnp.stack((masked(h_blocks, h_mask), masked(p1_blocks, p1_mask), masked(p_blocks, p_mask)), axis=1)
-    first, second = blocks[:, :, 0], blocks[:, :, 1]
-    own = jnp.stack((jnp.where(low, second, first), jnp.where(low, first, second)))
-    out_m, out_o = exchange(own)
-    pattern = p1_mask[:, 0][:, :, None, None].astype(jnp.bfloat16)
-
-    def placed(i):
-        m, o = out_m[:, i], out_o[:, i]
-        return (jnp.stack((jnp.where(low, o, m), jnp.where(low, m, o)), axis=1) * pattern)[:, None]
-
-    return placed(0), placed(1)
+    values = [v[:, 0] for v in (h_blocks, p1_blocks, p_blocks)]
+    masks = [v[:, 0].T for v in (h_mask, p1_mask, p_mask)]
+    return tuple(v[:, None] for v in exchange(values, masks))
 
 
 def solution(mesh):

time: 94.9 us -> 84.6 us (0.89)
  Pallas kernels: 86.8 us -> 80.8 us
  other arithmetic: 3.71 us -> 0 us
  local copies, waits for them, and re-layouts: 3.47 us -> 2.42 us
    pallas_call x1, Pallas kernels: 86.8 us -> 80.8 us  [exchange(): pl.pallas_call(kernel, out_shape=(jax.ShapeDtypeStruct((NM, 2) + block, j...]
    another operation x3 -> x0, other arithmetic: 2.26 us -> none  [the longest x1 1.22 us: placed(): jnp.stack((jnp.where(low, o, m), jnp.where(low, m, o)), axis=1) * pattern]
    mul x4 -> x0, other arithmetic: 1.38 us -> none  [the longest x2 1.2 us: masked(): return values[:, 0] * pattern[:, 0][:, :, None, None].astype(values.dtype)]
    unnamed x12 -> x4, local copies, waits for them, and re-layouts: 3.47 us -> 2.42 us
where the time goes in v2:
time: 84.6 us; the launch traced here: 83.9 us
  Pallas kernels  80.8 us (96%)
  local copies, waits for them, and re-layouts  2.42 us (3%)
    pallas_call x1, Pallas kernels, exchange(): pl.pallas_call(kernel, out_shape=(jax.ShapeDtypeStruct((NM, 2) + block, j...  80.8 us
    unnamed x4, local copies, waits for them, and re-layouts  2.42 us

profile of v2, /device:TPU:1, one launch (start us, length us, event | category | flops | bytes accessed | tf_op | source)
XLA Modules:
  0.0 83.9 jit_solution(9513403950887288663)
XLA Ops:
  0.6 80.8 %exchange.1 = (bf16[4,2,128,128]{3,2,1,0:T(8,128)(2,1)}, bf16[4,2,128,128]{3,2,1,0:T(8,128)(2,1)}) custom-call(bf16[4,2,128,128]{3,2,1,0:T(8,128)(2,1)} %bitcast.18, bf16[4,2,128,128]{3,2,1,0:T(8,128)(2,1)} %bitcast.19, bf16[4,2,128,128]{3,2,1,0:T(8,128)(2,1)} %bitcast.20, s32[2,4]{1,0:T(2,128)} %bitcast.23, s32[2,4]{1,0:T(2,128)} %bitcast.24, s32[2,4]{1,0:T(2,128)} %bitcast.25), custom_call_target="tpu_custom_call" | custom-call | tf_op jit(solution)/shard_map/exchange/pallas_call | solution.py:341
  81.5 0.0 copy-start
  81.5 1.7 %copy.12 = bf16[4,1,2,128,128]{4,3,2,1,0:T(8,128)(2,1)} copy(bf16[4,1,2,128,128]{4,3,2,1,0:T(8,128)(2,1)} %bitcast.22) | data formatting | bytes 524288
  83.2 0.0 copy-done
  83.2 0.7 copy.13
Async XLA Ops:
  81.5 1.7 %copy-start = (bf16[4,2,128,128]{3,2,1,0:T(8,128)(2,1)S(1)}, bf16[4,2,128,128]{3,2,1,0:T(8,128)(2,1)}, u32[]{:S(2)}) copy-start(bf16[4,2,128,128]{3,2,1,0:T(8,128)(2,1)} %get-tuple-element.5) | copy-start | bytes 786436

commit v3 on v2

--- a/solution.py
+++ b/solution.py
@@ -40,27 +40,29 @@
             src_ref=src, dst_ref=dst, send_sem=send, recv_sem=recv,
             device_id=device, device_id_type=MESH)
 
+    loads = [pltpu.make_async_copy(ref, raw.at[i], local_sem.at[i]) for i, ref in enumerate((h_ref, p1_ref, p_ref))]
+    for c in loads:
+        c.start()
     barrier = pltpu.get_barrier_semaphore()
     for peer in (dev_zu, dev_zd, dev_yu, dev_yd, dev_xu, dev_xd, dev_c):
         pl.semaphore_signal(barrier, inc=1, device_id=peer, device_id_type=MESH)
 
     slot_m = jnp.where(low, 1, 0)
     slots = (slot_m, 1 - slot_m)
-    loads = [pltpu.make_async_copy(ref, raw.at[i], local_sem.at[i]) for i, ref in enumerate((h_ref, p1_ref, p_ref))]
-    for c in loads:
-        c.start()
-    for m in range(NM):
-        acc[m] = jnp.zeros((2, 2, 128, 128), jnp.float32)
-    for i, (c, mask) in enumerate(zip(loads, (h_mask, p1_mask, p_mask))):
-        c.wait()
-        for kind in (M, O):
+    own = left.at[u]
+
+    def keep_own(kind):
+        for i, mask in enumerate((h_mask, p1_mask, p_mask)):
             for m in range(NM):
-                keep = mask[slots[kind], m].astype(jnp.float32)
-                block = (raw[i, m, slots[kind]].astype(jnp.float32) * keep).astype(jnp.bfloat16)
+                keep = jnp.full((128, 128), mask[slots[kind], m].astype(jnp.float32)).astype(jnp.bfloat16)
+                block = raw[i, m, slots[kind]] * keep
                 left[u, kind, m, i] = block
                 if kind == M:
                     strip[z, M, m, i] = block
-    own = left.at[u]
+
+    for c in loads:
+        c.wait()
+    keep_own(M)
     pl.semaphore_wait(barrier, 7)
 
     def z_copy(up, hop, kind, m):
@@ -73,8 +75,8 @@
         return remote(strip.at[origin, kind, m], strip.at[origin, kind, m],
                       z_send.at[0 if up else 1, 0, kind, m], z_recv.at[origin, kind, m], dev_c)
 
-    def z_round(hop, kind):
-        for m in range(NM):
+    def z_round(hop, kind, planes=range(NM)):
+        for m in planes:
             for up in (True, False):
                 limit = (UP_HOPS if up else DOWN_HOPS)[kind]
                 if hop <= limit:
@@ -85,6 +87,7 @@
     for m in range(NM):
         z_copy(True, 0, M, m).start()
         z_copy(False, 0, M, m).start()
+    keep_own(O)
 
     dev_f = (jnp.where(low, x_dn, x_up) * NZ + z, col)
     shift_up = jnp.where(x == NX - 1, 1, 0)
@@ -174,6 +177,9 @@
 
     side_f = jnp.where(low, 0, 1)
     far_sends(0, M, start)
+
+    for m in range(NM):
+        acc[m] = jnp.zeros((2, 2, 128, 128), jnp.float32)
 
     for m in range(NM):
         remote(strip.at[z, O, m], strip.at[z, O, m], f_send.at[m], z_recv.at[z, O, m], dev_c).wait_recv()
@@ -260,15 +266,8 @@
     far_pass(3, M)
     far_pass(1, M)
     far_pass(2, M)
-    z_round(3, O)
+    z_round(3, O, (0, 1))
     far_pass(2, O)
-
-    def third(i, _):
-        add(0, i // 2, (z + 3 + 2 * (i % 2)) % NZ)
-        return 0
-
-    lax.fori_loop(0, NM * 2, third, 0)
-
     f_keep.wait()
     for d in range(NY):
         who = ((y + d) % NY) * NC + 1 - k
@@ -279,6 +278,16 @@
                     spot = far.at[side, who, kind]
                     remote(spot, spot, q_send.at[side, d, kind], p_recv.at[side, who, kind], dev_c).wait_recv()
 
+    def far_near(i, _):
+        add(1, i // 5, (z + i % 5 + 6) % NZ)
+        return 0
+
+    lax.fori_loop(0, 10, far_near, 0)
+    z_round(3, O, (2,))
+    lax.fori_loop(10, 15, far_near, 0)
+    z_round(3, O, (3,))
+    lax.fori_loop(15, 20, far_near, 0)
+
     r_shift = jnp.where(low, shift_up, shift_dn)
     dev_r = (jnp.where(low, x_up, x_dn) * NZ + z, col)
 
@@ -292,11 +301,12 @@
         out_r[m, slots[kind]] = (s * keep).astype(jnp.bfloat16)
 
     for m in range(NM):
-        def early(i, _):
-            add(1, m, (z + i + 5) % NZ)
+        def third(i, _):
+            add(0, m, (z + 3 + 2 * i) % NZ)
+            add(1, m, (z + 3 + 2 * i) % NZ)
             return 0
 
-        lax.fori_loop(0, NZ - 1, early, 0)
+        lax.fori_loop(0, 2, third, 0)
         z_arrival(True, 4, M, m).wait_recv()
         z_arrival(False, 4, O, m).wait_recv()
         c, s = products(1, m, (z + 4) % NZ)
@@ -340,7 +350,7 @@
     block = (128, 128)
     return pl.pallas_call(
         kernel,
-        out_shape=(jax.ShapeDtypeStruct((NM, 2) + block, jnp.bfloat16),) * 2,
+        out_shape=(pltpu.VMEM((NM, 2) + block, jnp.bfloat16),) * 2,
         in_specs=[pl.BlockSpec(memory_space=pl.ANY)] * 3 + [pl.BlockSpec(memory_space=pltpu.SMEM)] * 3,
         out_specs=(pl.BlockSpec(memory_space=pltpu.VMEM),) * 2,
         scratch_shapes=[

time: 84.6 us -> 81 us (0.957)
  Pallas kernels: 80.8 us -> 78.5 us
  local copies, waits for them, and re-layouts: 2.42 us -> 1.41 us
    pallas_call x1, Pallas kernels: 80.8 us -> 78.5 us  [exchange(): pl.pallas_call(kernel, out_shape=(pltpu.VMEM((NM, 2) + block, jnp.bfloat1...]
    unnamed x4 -> x2, local copies, waits for them, and re-layouts: 2.42 us -> 1.41 us
where the time goes in v3:
time: 81 us; the launch traced here: 80.6 us
  Pallas kernels  78.5 us (97%)
  local copies, waits for them, and re-layouts  1.41 us (2%)
    pallas_call x1, Pallas kernels, exchange(): pl.pallas_call(kernel, out_shape=(pltpu.VMEM((NM, 2) + block, jnp.bfloat1...  78.5 us

profile of v3, /device:TPU:1, one launch (start us, length us, event | category | flops | bytes accessed | tf_op | source)
XLA Modules:
  0.0 80.6 jit_solution(12132060822765341220)
XLA Ops:
  0.6 78.5 %exchange.1 = (bf16[4,2,128,128]{3,2,1,0:T(8,128)(2,1)S(1)}, bf16[4,2,128,128]{3,2,1,0:T(8,128)(2,1)S(1)}) custom-call(bf16[4,2,128,128]{3,2,1,0:T(8,128)(2,1)} %bitcast.20, bf16[4,2,128,128]{3,2,1,0:T(8,128)(2,1)} %bitcast.21, bf16[4,2,128,128]{3,2,1,0:T(8,128)(2,1)} %bitcast.22, s32[2,4]{1,0:T(2,128)} %bitcast.23, s32[2,4]{1,0:T(2,128)} %bitcast.24, ...), custom_call_target="tpu_custom_call" | custom-call | tf_op jit(solution)/shard_map/exchange/pallas_call | solution.py:351
  79.2 0.7 copy.12
  79.9 0.7 copy.13

commit v4 on v3

--- a/solution.py
+++ b/solution.py
@@ -94,9 +94,9 @@
     shift_dn = jnp.where(x == 0, NM - 1, 0)
     f_shift = jnp.where(low, shift_dn, shift_up)
 
-    def f_copy(m):
-        there = (m + f_shift) % NM
-        return remote(own.at[O, m], strip.at[z, O, there], f_send.at[m], z_recv.at[z, O, there], dev_f)
+    def f_copy(there):
+        m = (there + NM - f_shift) % NM
+        return remote(own.at[O, m], strip.at[z, O, there], f_send.at[there], z_recv.at[z, O, there], dev_f)
 
     for m in range(NM):
         f_copy(m).start()
@@ -289,11 +289,12 @@
     lax.fori_loop(15, 20, far_near, 0)
 
     r_shift = jnp.where(low, shift_up, shift_dn)
+    b_shift = jnp.where(low, jnp.where(x == 0, 1, 0), jnp.where(x == NX - 1, NM - 1, 0))
     dev_r = (jnp.where(low, x_up, x_dn) * NZ + z, col)
 
     def r_copy(m):
         there = (m + r_shift) % NM
-        return remote(out_f.at[m], back.at[there], r_send.at[m], r_recv.at[there], dev_r)
+        return remote(out_f.at[m], back.at[there], r_send.at[m], r_recv.at[m], dev_r)
 
     def put(m, kind, c, s):
         keep = p1_mask[slots[kind], m].astype(jnp.float32)
@@ -316,8 +317,9 @@
         put(m, M, c + acc[m, 0, 0], s + acc[m, 0, 1])
         r_copy(m).start()
 
-    for m in range(NM):
-        remote(back.at[m], back.at[m], r_send.at[m], r_recv.at[m], dev_c).wait_recv()
+    for sent in range(NM):
+        m = (sent + b_shift) % NM
+        remote(back.at[m], back.at[m], r_send.at[sent], r_recv.at[sent], dev_c).wait_recv()
         put(m, O, back[m, 0].astype(jnp.float32), back[m, 1].astype(jnp.float32))
 
     for m in range(NM):
@@ -380,10 +382,32 @@
     )(*values, *masks)
 
 
+def write_out(c_ref, r_ref, oc, orr, sem):
+    a = pltpu.make_async_copy(c_ref, oc, sem.at[0])
+    b = pltpu.make_async_copy(r_ref, orr, sem.at[1])
+    a.start()
+    b.start()
+    a.wait()
+    b.wait()
+
+
+def finish(c, r):
+    c = pltpu.with_memory_space_constraint(c, pltpu.VMEM)
+    r = pltpu.with_memory_space_constraint(r, pltpu.VMEM)
+    return pl.pallas_call(
+        write_out,
+        out_shape=(jax.ShapeDtypeStruct(c.shape, c.dtype),) * 2,
+        in_specs=[pl.BlockSpec(memory_space=pltpu.VMEM)] * 2,
+        out_specs=(pl.BlockSpec(memory_space=pl.ANY),) * 2,
+        scratch_shapes=[pltpu.SemaphoreType.DMA((2,))],
+        name="finish",
+    )(c, r)
+
+
 def per_device(h_blocks, p_blocks, p1_blocks, h_mask, p_mask, p1_mask):
     values = [v[:, 0] for v in (h_blocks, p1_blocks, p_blocks)]
     masks = [v[:, 0].T for v in (h_mask, p1_mask, p_mask)]
-    return tuple(v[:, None] for v in exchange(values, masks))
+    return tuple(v[:, None] for v in finish(*exchange(values, masks)))
 
 
 def solution(mesh):

time: 81 us -> 78.4 us (0.968)
  local copies, waits for them, and re-layouts: 1.41 us -> 0 us
  Pallas kernels: 78.5 us -> 77.6 us
    pallas_call x1, Pallas kernels: 78.5 us -> 76.8 us  [exchange(): pl.pallas_call(kernel, out_shape=(pltpu.VMEM((NM, 2) + block, jnp.bfloat1...]
    unnamed x2 -> x0, local copies, waits for them, and re-layouts: 1.41 us -> none
where the time goes in v4:
time: 78.4 us; the launch traced here: 78.3 us
  Pallas kernels  77.6 us (99%)
    pallas_call x1, Pallas kernels, exchange(): pl.pallas_call(kernel, out_shape=(pltpu.VMEM((NM, 2) + block, jnp.bfloat1...  76.8 us

profile of v4, /device:TPU:1, one launch (start us, length us, event | category | flops | bytes accessed | tf_op | source)
XLA Modules:
  0.0 78.3 jit_solution(7455426602406295104)
XLA Ops:
  0.6 76.8 %exchange.1 = (bf16[4,2,128,128]{3,2,1,0:T(8,128)(2,1)S(1)}, bf16[4,2,128,128]{3,2,1,0:T(8,128)(2,1)S(1)}) custom-call(bf16[4,2,128,128]{3,2,1,0:T(8,128)(2,1)} %bitcast.18, bf16[4,2,128,128]{3,2,1,0:T(8,128)(2,1)} %bitcast.19, bf16[4,2,128,128]{3,2,1,0:T(8,128)(2,1)} %bitcast.20, s32[2,4]{1,0:T(2,128)} %bitcast.21, s32[2,4]{1,0:T(2,128)} %bitcast.22, ...), custom_call_target="tpu_custom_call" | custom-call | tf_op jit(solution)/shard_map/exchange/pallas_call | solution.py:353
  77.4 0.8 %finish.1 = (bf16[4,2,128,128]{3,2,1,0:T(8,128)(2,1)}, bf16[4,2,128,128]{3,2,1,0:T(8,128)(2,1)}) custom-call(bf16[4,2,128,128]{3,2,1,0:T(8,128)(2,1)S(1)} %get-tuple-element.6.c_ref, bf16[4,2,128,128]{3,2,1,0:T(8,128)(2,1)S(1)} %get-tuple-element.7.r_ref), custom_call_target="tpu_custom_call" | custom-call | tf_op jit(solution)/shard_map/finish/pallas_call | solution.py:397

commit v5 on v4

v5 whole, which is shorter than its diff:
```python
import functools

import jax
import jax.numpy as jnp
from jax import lax
from jax.experimental import pallas as pl
from jax.experimental.pallas import tpu as pltpu
from jax.sharding import PartitionSpec as P

MESH = pl.DeviceIdType.MESH
NX, NY, NZ, NC = 4, 4, 8, 2
NM = 4
M, O = 0, 1
UP_HOPS = (4, 3)
DOWN_HOPS = (3, 4)


FINE = ((False, 3, O), (True, 4, M), (False, 4, O))
WHOLE = tuple((up, hop, kind) for up in (True, False) for kind in (M, O)
              for hop in range(1, (UP_HOPS if up else DOWN_HOPS)[kind] + 1) if (up, hop, kind) not in FINE)


def kernel(h_ref, p1_ref, p_ref, h_hbm, p1_hbm, p_hbm, out_c, out_r,
           masks, raw, strip, left, far, out_f, back, acc,
           whole_recv, fine_recv, f_recv, l_recv, c_recv, p_recv, r_recv,
           z_send, y_send, c_send, f_send, p_send, q_send, fy_send, r_send, local_sem):
    row, col = lax.axis_index("row"), lax.axis_index("col")
    x, z = row // NZ, row % NZ
    y, k = col // NC, col % NC
    u = col
    low = z <= u
    x_up, x_dn = (x + 1) % NX, (x + NX - 1) % NX
    z_up, z_dn = (z + 1) % NZ, (z + NZ - 1) % NZ
    y_up, y_dn = (y + 1) % NY, (y + NY - 1) % NY

    def dev(x_=x, y_=y, z_=z, k_=k):
        return (x_ * NZ + z_, y_ * NC + k_)

    dev_zu, dev_zd = dev(z_=z_up), dev(z_=z_dn)
    dev_yu, dev_yd = dev(y_=y_up), dev(y_=y_dn)
    dev_xu, dev_xd = dev(x_=x_up), dev(x_=x_dn)
    dev_c = dev(k_=1 - k)

    def remote(src, dst, send, recv, device):
        return pltpu.make_async_remote_copy(
            src_ref=src, dst_ref=dst, send_sem=send, recv_sem=recv,
            device_id=device, device_id_type=MESH)

    for i, ref in enumerate((h_ref, p1_ref, p_ref)):
        pltpu.make_async_copy(ref, raw.at[i], local_sem.at[0]).start()
    for i, ref in enumerate((h_hbm, p1_hbm, p_hbm)):
        pltpu.make_async_copy(ref, masks.at[i], local_sem.at[1]).start()
    barrier = pltpu.get_barrier_semaphore()
    for peer in (dev_zu, dev_zd, dev_yu, dev_yd, dev_xu, dev_xd, dev_c):
        pl.semaphore_signal(barrier, inc=1, device_id=peer, device_id_type=MESH)

    slot_m = jnp.where(low, 1, 0)
    slots = (slot_m, 1 - slot_m)
    own = left.at[u]

    def keep_own(kind):
        for i in range(3):
            for m in range(NM):
                keep = jnp.full((128, 128), masks[i, slots[kind], m].astype(jnp.float32)).astype(jnp.bfloat16)
                block = raw[i, m, slots[kind]] * keep
                left[u, kind, m, i] = block
                if kind == M:
                    strip[z, M, m, i] = block

    pltpu.make_async_copy(masks, masks, local_sem.at[1]).wait()
    pltpu.make_async_copy(raw, raw, local_sem.at[0]).wait()
    keep_own(M)
    pl.semaphore_wait(barrier, 7)

    def z_from(up, hop):
        return (z - hop + NZ) % NZ if up else (z + hop) % NZ

    def z_sem(up, hop, kind, m):
        key = (up, hop, kind)
        return fine_recv.at[FINE.index(key), m] if key in FINE else whole_recv.at[WHOLE.index(key)]

    def z_copy(up, hop, kind, m):
        spot = strip.at[z_from(up, hop), kind, m]
        return remote(spot, spot, z_send, z_sem(up, hop + 1, kind, m), dev_zu if up else dev_zd)

    def z_wait(up, hop, kind, m=None):
        spot = strip.at[z_from(up, hop), kind] if m is None else strip.at[z_from(up, hop), kind, m]
        remote(spot, spot, z_send, z_sem(up, hop, kind, m), dev_c).wait_recv()

    def z_round(hop, kind, planes=range(NM)):
        for up in (True, False):
            limit = (UP_HOPS if up else DOWN_HOPS)[kind]
            if hop > limit:
                continue
            onward = hop < limit
            if (up, hop, kind) not in FINE and (0 if onward else NM - 1) in planes:
                z_wait(up, hop, kind)
            for m in planes:
                if (up, hop, kind) in FINE:
                    z_wait(up, hop, kind, m)
                if onward:
                    z_copy(up, hop, kind, m).start()

    for m in range(NM):
        z_copy(True, 0, M, m).start()
        z_copy(False, 0, M, m).start()
    keep_own(O)

    dev_f = (jnp.where(low, x_dn, x_up) * NZ + z, col)
    shift_up = jnp.where(x == NX - 1, 1, 0)
    shift_dn = jnp.where(x == 0, NM - 1, 0)
    f_shift = jnp.where(low, shift_dn, shift_up)

    def f_copy(there):
        m = (there + NM - f_shift) % NM
        return remote(own.at[O, m], strip.at[z, O, there], f_send, f_recv.at[there], dev_f)

    for m in range(NM):
        f_copy(m).start()

    def l_wait(d, kind):
        spot = left.at[((y + d) % NY) * NC + k, kind]
        remote(spot, spot, y_send, l_recv.at[d, kind], dev_c).wait_recv()

    def y_copy(up, kind, relay):
        if relay:
            who = (y_dn if up else y_up) * NC + k
            d = 2
        else:
            who = u
            d = 3 if up else 1
        spot = left.at[who, kind]
        return remote(spot, spot, y_send, l_recv.at[d, kind], dev_yu if up else dev_yd)

    y_relays = [y_copy(True, M, True), y_copy(False, O, True)]
    for up, kind in ((True, M), (False, O), (True, O), (False, M)):
        y_copy(up, kind, False).start()

    def c_copy(d, kind):
        spot = left.at[((y + d) % NY) * NC + k, kind]
        return remote(spot, spot, c_send, c_recv, dev_c)

    c_copy(0, M).start()
    c_copy(0, O).start()

    def far_wanted(side, who, kind, at):
        if side == 0:
            inside = who >= z if kind == O else who <= 2 * at + 1
            return jnp.logical_and(2 * at + 1 >= z, inside)
        inside = who < z if kind == O else who > 2 * at
        return jnp.logical_and(2 * at < z, inside)

    def twin(side, who, kind):
        return jnp.logical_and(who == 2 * y + 1, side == 1 and kind == M)

    def far_recv(side, who, kind):
        return p_recv.at[jnp.where(twin(side, who, kind), 16, kind * 8 + who)]

    def far_send(sems, side, d, kind):
        who = ((y + d) % NY) * NC + k
        return sems.at[jnp.where(twin(side, who, kind), 8, kind * NY + d)]

    def far_by_x(side, d, kind):
        home = (y + d) % NY
        who = home * NC + k
        wanted = far_wanted(side, who, kind, y)
        if d in (1, 3):
            wanted = jnp.logical_and(wanted, jnp.logical_not(far_wanted(side, who, kind, home)))
        return wanted

    def far_sends(d, kind, go=True):
        who = ((y + d) % NY) * NC + k
        src = left.at[who, kind]
        for side in (0, 1):
            @pl.when(far_by_x(side, d, kind))
            def _():
                sems = far_send(p_send, side, d, kind), far_recv(side, who, kind)
                if not go:
                    remote(src, src, *sems, dev_xd).wait_send()
                    return
                shift = shift_dn if side == 0 else shift_up
                for m in range(NM):
                    remote(src.at[m], far.at[side, who, kind, (m + shift) % NM], *sems,
                           dev_xd if side == 0 else dev_xu).start()

    def far_y(kind, act):
        for side in (0, 1):
            for way, (there, device) in enumerate(((y_up, dev_yu), (y_dn, dev_yd))):
                @pl.when(jnp.logical_and(far_wanted(side, u, kind, y), far_wanted(side, u, kind, there)))
                def _():
                    src = strip.at[z, O] if kind == O else far.at[side, u, M]
                    act(remote(src, far.at[side, u, kind], fy_send.at[way, kind],
                               p_recv.at[kind * 8 + u], device))

    def far_pass(d, kind):
        who = ((y + d) % NY) * NC + k
        for side in (0, 1):
            @pl.when(far_wanted(side, who, kind, y))
            def _():
                spot = far.at[side, who, kind]
                copy = remote(spot, spot, far_send(q_send, side, d, kind), far_recv(side, who, kind), dev_c)
                copy.wait_recv()
                copy.start()

    def start(c):
        c.start()

    side_f = jnp.where(low, 0, 1)
    far_sends(0, M)

    for m in range(NM):
        acc[m] = jnp.zeros((2, 2, 128, 128), jnp.float32)

    for m in range(NM):
        remote(strip.at[z, O, m], strip.at[z, O, m], f_send, f_recv.at[m], dev_c).wait_recv()
        z_copy(True, 0, O, m).start()
        z_copy(False, 0, O, m).start()
    f_keep = pltpu.make_async_copy(strip.at[z, O], far.at[side_f, u, O], local_sem.at[2])
    f_keep.start()
    f_pass = remote(strip.at[z, O], far.at[side_f, u, O], local_sem.at[3], p_recv.at[8 + u], dev_c)
    f_pass.start()

    l_wait(3, M)
    y_relays[0].start()
    far_sends(3, M)
    c_copy(3, M).start()
    l_wait(1, O)
    y_relays[1].start()
    far_sends(1, O)
    c_copy(1, O).start()
    far_y(O, start)

    z_round(1, M)

    l_wait(3, O)
    far_sends(3, O)
    c_copy(3, O).start()
    l_wait(1, M)
    far_sends(1, M)
    c_copy(1, M).start()

    far_pass(0, M)
    far_y(M, start)
    z_round(1, O)
    z_round(2, M)

    l_wait(2, M)
    far_sends(2, M)
    c_copy(2, M).start()
    l_wait(2, O)
    far_sends(2, O)
    c_copy(2, O).start()

    z_round(2, O)
    far_pass(3, O)
    far_pass(1, O)

    zero = jnp.zeros((128, 128), jnp.bfloat16)

    def products(r, m, zp):
        hm, am, pm = (strip[zp, M, m, i] for i in range(3))
        hf, af, pf = (strip[zp, O, m, i] for i in range(3))
        if r == 0:
            ok = jnp.where(zp > u, zp >= z, zp < z)
            first = [left[zp, M, m, i] for i in range(3)]
            second = [jnp.where(ok, left[zp, O, m, i], zero) for i in range(3)]
        else:
            ok_m = jnp.where(low, zp >= z, zp < z)
            ok_f = (zp <= u) == low
            first = [jnp.where(ok_m, far[side_f, zp, O, m, i], zero) for i in range(3)]
            second = [jnp.where(ok_f, far[side_f, zp, M, m, i], zero) for i in range(3)]
        lh, la, lp = (jnp.concatenate([f, s], axis=1) for f, s in zip(first, second))
        one = jnp.dot(jnp.concatenate([lh, lp], axis=0), jnp.concatenate([am, af], axis=0),
                      preferred_element_type=jnp.float32)
        rhs = jnp.concatenate([jnp.concatenate([-hm, pm], axis=1), jnp.concatenate([-hf, pf], axis=1)], axis=0)
        two = jnp.dot(la, rhs, preferred_element_type=jnp.float32)
        return one[:128] + two[:, :128], one[128:] + two[:, 128:]

    def add(r, m, zp):
        c, s = products(r, m, zp)
        acc[m, r, 0] += c
        acc[m, r, 1] += s

    halves = left.at[pl.ds(0, NY)]
    remote(halves, halves, c_send, c_recv, dev_c).wait_recv()

    def near(i, _):
        add(0, i // 5, (z + i % 5 + 6) % NZ)
        return 0

    lax.fori_loop(0, NM * 5, near, 0)

    z_round(3, M)
    far_pass(3, M)
    far_pass(1, M)
    far_pass(2, M)
    z_round(3, O, (0, 1))
    far_pass(2, O)
    f_keep.wait()
    for d in range(NY):
        who = ((y + d) % NY) * NC + 1 - k
        for kind in (M, O):
            for side in (0, 1):
                @pl.when(far_wanted(side, who, kind, y))
                def _():
                    spot = far.at[side, who, kind]
                    remote(spot, spot, q_send.at[0], far_recv(side, who, kind), dev_c).wait_recv()

    def far_near(i, _):
        add(1, i // 5, (z + i % 5 + 6) % NZ)
        return 0

    lax.fori_loop(0, 10, far_near, 0)
    z_round(3, O, (2,))
    lax.fori_loop(10, 15, far_near, 0)
    z_round(3, O, (3,))
    lax.fori_loop(15, 20, far_near, 0)

    r_shift = jnp.where(low, shift_up, shift_dn)
    b_shift = jnp.where(low, jnp.where(x == 0, 1, 0), jnp.where(x == NX - 1, NM - 1, 0))
    dev_r = (jnp.where(low, x_up, x_dn) * NZ + z, col)

    def r_copy(m):
        there = (m + r_shift) % NM
        return remote(out_f.at[m], back.at[there], r_send, r_recv.at[m], dev_r)

    def put(m, kind, c, s):
        keep = masks[1, slots[kind], m].astype(jnp.float32)
        out_c[m, slots[kind]] = (c * keep).astype(jnp.bfloat16)
        out_r[m, slots[kind]] = (s * keep).astype(jnp.bfloat16)

    for m in range(NM):
        def third(i, _):
            add(0, m, (z + 3 + 2 * i) % NZ)
            add(1, m, (z + 3 + 2 * i) % NZ)
            return 0

        lax.fori_loop(0, 2, third, 0)
        z_wait(True, 4, M, m)
        z_wait(False, 4, O, m)
        c, s = products(1, m, (z + 4) % NZ)
        out_f[m, 0] = (c + acc[m, 1, 0]).astype(jnp.bfloat16)
        out_f[m, 1] = (s + acc[m, 1, 1]).astype(jnp.bfloat16)
        c, s = products(0, m, (z + 4) % NZ)
        put(m, M, c + acc[m, 0, 0], s + acc[m, 0, 1])
        r_copy(m).start()

    for sent in range(NM):
        m = (sent + b_shift) % NM
        remote(back.at[m], back.at[m], r_send, r_recv.at[sent], dev_c).wait_recv()
        put(m, O, back[m, 0].astype(jnp.float32), back[m, 1].astype(jnp.float32))

    def sent_all(ref, sem):
        remote(ref, ref, sem, r_recv.at[0], dev_c).wait_send()

    sent_all(strip.at[pl.ds(0, NZ - 1)], z_send)
    sent_all(left.at[pl.ds(0, 3)], y_send)
    sent_all(left.at[pl.ds(0, NY)], c_send)
    sent_all(strip.at[0, O], f_send)
    sent_all(out_f, r_send)
    sent_all(strip.at[0, O], local_sem.at[3])
    far_y(M, lambda c: c.wait_send())
    far_y(O, lambda c: c.wait_send())
    for d in range(NY):
        who = ((y + d) % NY) * NC + k
        for kind in (M, O):
            if (d, kind) != (0, O):
                far_sends(d, kind, False)
                for side in (0, 1):
                    @pl.when(far_wanted(side, who, kind, y))
                    def _():
                        sent_all(far.at[side, who, kind], far_send(q_send, side, d, kind))


def exchange(values, masks):
    dma = pltpu.SemaphoreType.DMA
    block = (128, 128)
    return pl.pallas_call(
        kernel,
        out_shape=(pltpu.VMEM((NM, 2) + block, jnp.bfloat16),) * 2,
        in_specs=[pl.BlockSpec(memory_space=pl.ANY)] * 6,
        out_specs=(pl.BlockSpec(memory_space=pltpu.VMEM),) * 2,
        scratch_shapes=[
            pltpu.SMEM((3, 2, NM), jnp.int32),
            pltpu.VMEM((3, NM, 2) + block, jnp.bfloat16),
            pltpu.VMEM((NZ, 2, NM, 3) + block, jnp.bfloat16),
            pltpu.VMEM((8, 2, NM, 3) + block, jnp.bfloat16),
            pltpu.VMEM((2, 8, 2, NM, 3) + block, jnp.bfloat16),
            pltpu.VMEM((NM, 2) + block, jnp.bfloat16),
            pltpu.VMEM((NM, 2) + block, jnp.bfloat16),
            pltpu.VMEM((NM, 2, 2) + block, jnp.float32),
            dma((len(WHOLE),)),
            dma((len(FINE), NM)),
            dma((NM,)),
            dma((NY, 2)),
            dma(()),
            dma((17,)),
            dma((NM,)),
            dma(()),
            dma(()),
            dma(()),
            dma(()),
            dma((9,)),
            dma((9,)),
            dma((2, 2)),
            dma(()),
            dma((4,)),
        ],
        compiler_params=pltpu.CompilerParams(collective_id=0, has_side_effects=True),
        name="exchange",
    )(*values, *masks)


def write_out(c_ref, r_ref, oc, orr, sem):
    a = pltpu.make_async_copy(c_ref, oc, sem.at[0])
    b = pltpu.make_async_copy(r_ref, orr, sem.at[1])
    a.start()
    b.start()
    a.wait()
    b.wait()


def finish(c, r):
    c = pltpu.with_memory_space_constraint(c, pltpu.VMEM)
    r = pltpu.with_memory_space_constraint(r, pltpu.VMEM)
    return pl.pallas_call(
        write_out,
        out_shape=(jax.ShapeDtypeStruct(c.shape, c.dtype),) * 2,
        in_specs=[pl.BlockSpec(memory_space=pltpu.VMEM)] * 2,
        out_specs=(pl.BlockSpec(memory_space=pl.ANY),) * 2,
        scratch_shapes=[pltpu.SemaphoreType.DMA((2,))],
        name="finish",
    )(c, r)


def per_device(h_blocks, p_blocks, p1_blocks, h_mask, p_mask, p1_mask):
    values = [v[:, 0] for v in (h_blocks, p1_blocks, p_blocks)]
    masks = [v[:, 0].T for v in (h_mask, p1_mask, p_mask)]
    return tuple(v[:, None] for v in finish(*exchange(values, masks)))


def solution(mesh):
    blocks = P(None, "row", "col", None, None)
    masks = P(None, "row", "col")
    return jax.shard_map(
        per_device, mesh=mesh, in_specs=(blocks,) * 3 + (masks,) * 3,
        out_specs=(blocks, blocks), check_vma=False,
    )
```

time: 78.4 us -> 75.6 us (0.964)
  Pallas kernels: 77.6 us -> 74.9 us
    pallas_call x1, Pallas kernels: 76.8 us -> 74.1 us  [exchange(): pl.pallas_call(kernel, out_shape=(pltpu.VMEM((NM, 2) + block, jnp.bfloat1...]
where the time goes in v5:
time: 75.6 us; the launch traced here: 75.5 us
  Pallas kernels  74.9 us (99%)
    pallas_call x1, Pallas kernels, exchange(): pl.pallas_call(kernel, out_shape=(pltpu.VMEM((NM, 2) + block, jnp.bfloat1...  74.1 us

profile of v5, /device:TPU:1, one launch (start us, length us, event | category | flops | bytes accessed | tf_op | source)
XLA Modules:
  0.0 75.5 jit_solution(17667085911807003492)
XLA Ops:
  0.6 74.1 %exchange.1 = (bf16[4,2,128,128]{3,2,1,0:T(8,128)(2,1)S(1)}, bf16[4,2,128,128]{3,2,1,0:T(8,128)(2,1)S(1)}) custom-call(bf16[4,2,128,128]{3,2,1,0:T(8,128)(2,1)} %bitcast.18, bf16[4,2,128,128]{3,2,1,0:T(8,128)(2,1)} %bitcast.19, bf16[4,2,128,128]{3,2,1,0:T(8,128)(2,1)} %bitcast.20, s32[2,4]{1,0:T(2,128)} %bitcast.21, s32[2,4]{1,0:T(2,128)} %bitcast.22, ...), custom_call_target="tpu_custom_call" | custom-call | tf_op jit(solution)/shard_map/exchange/pallas_call | solution.py:378
  74.7 0.8 %finish.1 = (bf16[4,2,128,128]{3,2,1,0:T(8,128)(2,1)}, bf16[4,2,128,128]{3,2,1,0:T(8,128)(2,1)}) custom-call(bf16[4,2,128,128]{3,2,1,0:T(8,128)(2,1)S(1)} %get-tuple-element.6.c_ref, bf16[4,2,128,128]{3,2,1,0:T(8,128)(2,1)S(1)} %get-tuple-element.7.r_ref), custom_call_target="tpu_custom_call" | custom-call | tf_op jit(solution)/shard_map/finish/pallas_call | solution.py:426

commit v6 on v5

--- a/solution.py
+++ b/solution.py
@@ -16,13 +16,14 @@
 
 
 FINE = ((False, 3, O), (True, 4, M), (False, 4, O))
+LAST = FINE[1:]
 WHOLE = tuple((up, hop, kind) for up in (True, False) for kind in (M, O)
               for hop in range(1, (UP_HOPS if up else DOWN_HOPS)[kind] + 1) if (up, hop, kind) not in FINE)
 
 
 def kernel(h_ref, p1_ref, p_ref, h_hbm, p1_hbm, p_hbm, out_c, out_r,
            masks, raw, strip, left, far, out_f, back, acc,
-           whole_recv, fine_recv, f_recv, l_recv, c_recv, p_recv, r_recv,
+           whole_recv, fine_recv, last_recv, f_recv, l_recv, c_recv, p_recv, r_recv,
            z_send, y_send, c_send, f_send, p_send, q_send, fy_send, r_send, local_sem):
     row, col = lax.axis_index("row"), lax.axis_index("col")
     x, z = row // NZ, row % NZ
@@ -86,6 +87,12 @@
     def z_wait(up, hop, kind, m=None):
         spot = strip.at[z_from(up, hop), kind] if m is None else strip.at[z_from(up, hop), kind, m]
         remote(spot, spot, z_send, z_sem(up, hop, kind, m), dev_c).wait_recv()
+
+    def z_part(up, part, hop=3):
+        kind = M if up else O
+        spot = strip.at[z_from(up, hop), kind, NM - 1, pl.ds(2 * part, 2 - part)]
+        sem = fine_recv.at[1 if up else 2, NM - 1] if part == 0 else last_recv.at[0 if up else 1]
+        return remote(spot, spot, z_send, sem, dev_zu if up else dev_zd)
 
     def z_round(hop, kind, planes=range(NM)):
         for up in (True, False):
@@ -98,7 +105,10 @@
             for m in planes:
                 if (up, hop, kind) in FINE:
                     z_wait(up, hop, kind, m)
-                if onward:
+                if onward and m == NM - 1 and (up, hop + 1, kind) in LAST:
+                    z_part(up, 0).start()
+                    z_part(up, 1).start()
+                elif onward:
                     z_copy(up, hop, kind, m).start()
 
     for m in range(NM):
@@ -257,24 +267,35 @@
 
     zero = jnp.zeros((128, 128), jnp.bfloat16)
 
+    def sides(r, m, zp, which):
+        if r == 0:
+            ok = jnp.where(zp > u, zp >= z, zp < z)
+            first = {i: left[zp, M, m, i] for i in which}
+            second = {i: jnp.where(ok, left[zp, O, m, i], zero) for i in which}
+        else:
+            ok_m = jnp.where(low, zp >= z, zp < z)
+            ok_f = (zp <= u) == low
+            first = {i: jnp.where(ok_m, far[side_f, zp, O, m, i], zero) for i in which}
+            second = {i: jnp.where(ok_f, far[side_f, zp, M, m, i], zero) for i in which}
+        return {i: jnp.concatenate([first[i], second[i]], axis=1) for i in which}
+
     def products(r, m, zp):
         hm, am, pm = (strip[zp, M, m, i] for i in range(3))
         hf, af, pf = (strip[zp, O, m, i] for i in range(3))
-        if r == 0:
-            ok = jnp.where(zp > u, zp >= z, zp < z)
-            first = [left[zp, M, m, i] for i in range(3)]
-            second = [jnp.where(ok, left[zp, O, m, i], zero) for i in range(3)]
-        else:
-            ok_m = jnp.where(low, zp >= z, zp < z)
-            ok_f = (zp <= u) == low
-            first = [jnp.where(ok_m, far[side_f, zp, O, m, i], zero) for i in range(3)]
-            second = [jnp.where(ok_f, far[side_f, zp, M, m, i], zero) for i in range(3)]
-        lh, la, lp = (jnp.concatenate([f, s], axis=1) for f, s in zip(first, second))
-        one = jnp.dot(jnp.concatenate([lh, lp], axis=0), jnp.concatenate([am, af], axis=0),
+        lhs = sides(r, m, zp, (0, 1, 2))
+        one = jnp.dot(jnp.concatenate([lhs[0], lhs[2]], axis=0), jnp.concatenate([am, af], axis=0),
                       preferred_element_type=jnp.float32)
         rhs = jnp.concatenate([jnp.concatenate([-hm, pm], axis=1), jnp.concatenate([-hf, pf], axis=1)], axis=0)
-        two = jnp.dot(la, rhs, preferred_element_type=jnp.float32)
+        two = jnp.dot(lhs[1], rhs, preferred_element_type=jnp.float32)
         return one[:128] + two[:, :128], one[128:] + two[:, 128:]
+
+    def one_product(r, m, zp, i):
+        lhs = sides(r, m, zp, (i, 1))
+        bm, am, bf, af = strip[zp, M, m, i], strip[zp, M, m, 1], strip[zp, O, m, i], strip[zp, O, m, 1]
+        if i == 0:
+            bm, bf = -bm, -bf
+        return jnp.dot(jnp.concatenate([lhs[i], lhs[1]], axis=1), jnp.concatenate([am, af, bm, bf], axis=0),
+                       preferred_element_type=jnp.float32)
 
     def add(r, m, zp):
         c, s = products(r, m, zp)
@@ -324,6 +345,10 @@
         there = (m + r_shift) % NM
         return remote(out_f.at[m], back.at[there], r_send, r_recv.at[m], dev_r)
 
+    def r_part(i):
+        there = (NM - 1 + r_shift) % NM
+        return remote(out_f.at[NM - 1, i], back.at[there, i], r_send, r_recv.at[NM - 1 + i], dev_r)
+
     def put(m, kind, c, s):
         keep = masks[1, slots[kind], m].astype(jnp.float32)
         out_c[m, slots[kind]] = (c * keep).astype(jnp.bfloat16)
@@ -336,18 +361,33 @@
             return 0
 
         lax.fori_loop(0, 2, third, 0)
-        z_wait(True, 4, M, m)
-        z_wait(False, 4, O, m)
-        c, s = products(1, m, (z + 4) % NZ)
-        out_f[m, 0] = (c + acc[m, 1, 0]).astype(jnp.bfloat16)
-        out_f[m, 1] = (s + acc[m, 1, 1]).astype(jnp.bfloat16)
-        c, s = products(0, m, (z + 4) % NZ)
-        put(m, M, c + acc[m, 0, 0], s + acc[m, 0, 1])
-        r_copy(m).start()
+        opposite = (z + 4) % NZ
+        if m < NM - 1:
+            z_wait(True, 4, M, m)
+            z_wait(False, 4, O, m)
+            c, s = products(1, m, opposite)
+            out_f[m, 0] = (c + acc[m, 1, 0]).astype(jnp.bfloat16)
+            out_f[m, 1] = (s + acc[m, 1, 1]).astype(jnp.bfloat16)
+            c, s = products(0, m, opposite)
+            put(m, M, c + acc[m, 0, 0], s + acc[m, 0, 1])
+            r_copy(m).start()
+        else:
+            total = []
+            for i in range(2):
+                for up in (True, False):
+                    z_part(up, i, 4).wait_recv()
+                out_f[m, i] = (one_product(1, m, opposite, 2 * i) + acc[m, 1, i]).astype(jnp.bfloat16)
+                total.append(one_product(0, m, opposite, 2 * i) + acc[m, 0, i])
+                r_part(i).start()
+            put(m, M, *total)
 
     for sent in range(NM):
         m = (sent + b_shift) % NM
-        remote(back.at[m], back.at[m], r_send, r_recv.at[sent], dev_c).wait_recv()
+        if sent < NM - 1:
+            remote(back.at[m], back.at[m], r_send, r_recv.at[sent], dev_c).wait_recv()
+        else:
+            for i in range(2):
+                remote(back.at[m, i], back.at[m, i], r_send, r_recv.at[sent + i], dev_c).wait_recv()
         put(m, O, back[m, 0].astype(jnp.float32), back[m, 1].astype(jnp.float32))
 
     def sent_all(ref, sem):
@@ -391,11 +431,12 @@
             pltpu.VMEM((NM, 2, 2) + block, jnp.float32),
             dma((len(WHOLE),)),
             dma((len(FINE), NM)),
+            dma((2,)),
             dma((NM,)),
             dma((NY, 2)),
             dma(()),
             dma((17,)),
-            dma((NM,)),
+            dma((NM + 1,)),
             dma(()),
             dma(()),
             dma(()),

time: 75.6 us -> 74.9 us (level)
  Pallas kernels: 74.9 us -> 74.1 us
where the time goes in v6:
time: 74.9 us; the launch traced here: 74.8 us
  Pallas kernels  74.1 us (99%)
    pallas_call x1, Pallas kernels, exchange(): pl.pallas_call(kernel, out_shape=(pltpu.VMEM((NM, 2) + block, jnp.bfloat1...  73.3 us

profile of v6, /device:TPU:1, one launch (start us, length us, event | category | flops | bytes accessed | tf_op | source)
XLA Modules:
  0.0 74.8 jit_solution(14593817808601142794)
XLA Ops:
  0.6 73.3 %exchange.1 = (bf16[4,2,128,128]{3,2,1,0:T(8,128)(2,1)S(1)}, bf16[4,2,128,128]{3,2,1,0:T(8,128)(2,1)S(1)}) custom-call(bf16[4,2,128,128]{3,2,1,0:T(8,128)(2,1)} %bitcast.18, bf16[4,2,128,128]{3,2,1,0:T(8,128)(2,1)} %bitcast.19, bf16[4,2,128,128]{3,2,1,0:T(8,128)(2,1)} %bitcast.20, s32[2,4]{1,0:T(2,128)} %bitcast.21, s32[2,4]{1,0:T(2,128)} %bitcast.22, ...), custom_call_target="tpu_custom_call" | custom-call | tf_op jit(solution)/shard_map/exchange/pallas_call | solution.py:418
  74.0 0.8 %finish.1 = (bf16[4,2,128,128]{3,2,1,0:T(8,128)(2,1)}, bf16[4,2,128,128]{3,2,1,0:T(8,128)(2,1)}) custom-call(bf16[4,2,128,128]{3,2,1,0:T(8,128)(2,1)S(1)} %get-tuple-element.6.c_ref, bf16[4,2,128,128]{3,2,1,0:T(8,128)(2,1)S(1)} %get-tuple-element.7.r_ref), custom_call_target="tpu_custom_call" | custom-call | tf_op jit(solution)/shard_map/finish/pallas_call | solution.py:467

commit v7 on v6

--- a/solution.py
+++ b/solution.py
@@ -130,7 +130,7 @@
 
     def l_wait(d, kind):
         spot = left.at[((y + d) % NY) * NC + k, kind]
-        remote(spot, spot, y_send, l_recv.at[d, kind], dev_c).wait_recv()
+        remote(spot, spot, y_send, l_recv.at[d - 1, kind], dev_c).wait_recv()
 
     def y_copy(up, kind, relay):
         if relay:
@@ -140,7 +140,7 @@
             who = u
             d = 3 if up else 1
         spot = left.at[who, kind]
-        return remote(spot, spot, y_send, l_recv.at[d, kind], dev_yu if up else dev_yd)
+        return remote(spot, spot, y_send, l_recv.at[d - 1, kind], dev_yu if up else dev_yd)
 
     y_relays = [y_copy(True, M, True), y_copy(False, O, True)]
     for up, kind in ((True, M), (False, O), (True, O), (False, M)):
@@ -381,15 +381,6 @@
                 r_part(i).start()
             put(m, M, *total)
 
-    for sent in range(NM):
-        m = (sent + b_shift) % NM
-        if sent < NM - 1:
-            remote(back.at[m], back.at[m], r_send, r_recv.at[sent], dev_c).wait_recv()
-        else:
-            for i in range(2):
-                remote(back.at[m, i], back.at[m, i], r_send, r_recv.at[sent + i], dev_c).wait_recv()
-        put(m, O, back[m, 0].astype(jnp.float32), back[m, 1].astype(jnp.float32))
-
     def sent_all(ref, sem):
         remote(ref, ref, sem, r_recv.at[0], dev_c).wait_send()
 
@@ -397,7 +388,6 @@
     sent_all(left.at[pl.ds(0, 3)], y_send)
     sent_all(left.at[pl.ds(0, NY)], c_send)
     sent_all(strip.at[0, O], f_send)
-    sent_all(out_f, r_send)
     sent_all(strip.at[0, O], local_sem.at[3])
     far_y(M, lambda c: c.wait_send())
     far_y(O, lambda c: c.wait_send())
@@ -410,6 +400,16 @@
                     @pl.when(far_wanted(side, who, kind, y))
                     def _():
                         sent_all(far.at[side, who, kind], far_send(q_send, side, d, kind))
+
+    for sent in range(NM):
+        m = (sent + b_shift) % NM
+        if sent < NM - 1:
+            remote(back.at[m], back.at[m], r_send, r_recv.at[sent], dev_c).wait_recv()
+        else:
+            for i in range(2):
+                remote(back.at[m, i], back.at[m, i], r_send, r_recv.at[sent + i], dev_c).wait_recv()
+        put(m, O, back[m, 0].astype(jnp.float32), back[m, 1].astype(jnp.float32))
+    sent_all(out_f, r_send)
 
 
 def exchange(values, masks):
@@ -433,7 +433,7 @@
             dma((len(FINE), NM)),
             dma((2,)),
             dma((NM,)),
-            dma((NY, 2)),
+            dma((NY - 1, 2)),
             dma(()),
             dma((17,)),
             dma((NM + 1,)),

time: 74.9 us -> 74.8 us (level)
  no operation moved by 1% of the time
where the time goes in v7:
time: 74.8 us; the launch traced here: 74.6 us
  Pallas kernels  74 us (99%)
    pallas_call x1, Pallas kernels, exchange(): pl.pallas_call(kernel, out_shape=(pltpu.VMEM((NM, 2) + block, jnp.bfloat1...  73.2 us

profile of v7, /device:TPU:1, one launch (start us, length us, event | category | flops | bytes accessed | tf_op | source)
XLA Modules:
  0.0 74.6 jit_solution(13703673200462878184)
XLA Ops:
  0.6 73.2 %exchange.1 = (bf16[4,2,128,128]{3,2,1,0:T(8,128)(2,1)S(1)}, bf16[4,2,128,128]{3,2,1,0:T(8,128)(2,1)S(1)}) custom-call(bf16[4,2,128,128]{3,2,1,0:T(8,128)(2,1)} %bitcast.18, bf16[4,2,128,128]{3,2,1,0:T(8,128)(2,1)} %bitcast.19, bf16[4,2,128,128]{3,2,1,0:T(8,128)(2,1)} %bitcast.20, s32[2,4]{1,0:T(2,128)} %bitcast.21, s32[2,4]{1,0:T(2,128)} %bitcast.22, ...), custom_call_target="tpu_custom_call" | custom-call | tf_op jit(solution)/shard_map/exchange/pallas_call | solution.py:418
  73.8 0.8 %finish.1 = (bf16[4,2,128,128]{3,2,1,0:T(8,128)(2,1)}, bf16[4,2,128,128]{3,2,1,0:T(8,128)(2,1)}) custom-call(bf16[4,2,128,128]{3,2,1,0:T(8,128)(2,1)S(1)} %get-tuple-element.6.c_ref, bf16[4,2,128,128]{3,2,1,0:T(8,128)(2,1)S(1)} %get-tuple-element.7.r_ref), custom_call_target="tpu_custom_call" | custom-call | tf_op jit(solution)/shard_map/finish/pallas_call | solution.py:467

commit v8 on v7

--- a/solution.py
+++ b/solution.py
@@ -166,9 +166,13 @@
     def far_recv(side, who, kind):
         return p_recv.at[jnp.where(twin(side, who, kind), 16, kind * 8 + who)]
 
-    def far_send(sems, side, d, kind):
-        who = ((y + d) % NY) * NC + k
-        return sems.at[jnp.where(twin(side, who, kind), 8, kind * NY + d)]
+    def wait_count(conditions, sem):
+        count = sum(jnp.where(c, 1, 0) for c in conditions)
+        for n in range(1, 9):
+            @pl.when(count == n)
+            def _():
+                some = far.at[0, pl.ds(0, n), M]
+                remote(some, some, sem, f_recv.at[0], dev_c).wait_send()
 
     def far_by_x(side, d, kind):
         home = (y + d) % NY
@@ -178,29 +182,27 @@
             wanted = jnp.logical_and(wanted, jnp.logical_not(far_wanted(side, who, kind, home)))
         return wanted
 
-    def far_sends(d, kind, go=True):
+    def far_sends(d, kind):
         who = ((y + d) % NY) * NC + k
         src = left.at[who, kind]
         for side in (0, 1):
             @pl.when(far_by_x(side, d, kind))
             def _():
-                sems = far_send(p_send, side, d, kind), far_recv(side, who, kind)
-                if not go:
-                    remote(src, src, *sems, dev_xd).wait_send()
-                    return
                 shift = shift_dn if side == 0 else shift_up
                 for m in range(NM):
-                    remote(src.at[m], far.at[side, who, kind, (m + shift) % NM], *sems,
+                    remote(src.at[m], far.at[side, who, kind, (m + shift) % NM], p_send, far_recv(side, who, kind),
                            dev_xd if side == 0 else dev_xu).start()
 
-    def far_y(kind, act):
+    def far_by_y(side, kind, there):
+        return jnp.logical_and(far_wanted(side, u, kind, y), far_wanted(side, u, kind, there))
+
+    def far_y(kind):
         for side in (0, 1):
-            for way, (there, device) in enumerate(((y_up, dev_yu), (y_dn, dev_yd))):
-                @pl.when(jnp.logical_and(far_wanted(side, u, kind, y), far_wanted(side, u, kind, there)))
+            for there, device in ((y_up, dev_yu), (y_dn, dev_yd)):
+                @pl.when(far_by_y(side, kind, there))
                 def _():
                     src = strip.at[z, O] if kind == O else far.at[side, u, M]
-                    act(remote(src, far.at[side, u, kind], fy_send.at[way, kind],
-                               p_recv.at[kind * 8 + u], device))
+                    remote(src, far.at[side, u, kind], fy_send, p_recv.at[kind * 8 + u], device).start()
 
     def far_pass(d, kind):
         who = ((y + d) % NY) * NC + k
@@ -208,12 +210,9 @@
             @pl.when(far_wanted(side, who, kind, y))
             def _():
                 spot = far.at[side, who, kind]
-                copy = remote(spot, spot, far_send(q_send, side, d, kind), far_recv(side, who, kind), dev_c)
+                copy = remote(spot, spot, q_send, far_recv(side, who, kind), dev_c)
                 copy.wait_recv()
                 copy.start()
-
-    def start(c):
-        c.start()
 
     side_f = jnp.where(low, 0, 1)
     far_sends(0, M)
@@ -238,7 +237,7 @@
     y_relays[1].start()
     far_sends(1, O)
     c_copy(1, O).start()
-    far_y(O, start)
+    far_y(O)
 
     z_round(1, M)
 
@@ -250,7 +249,7 @@
     c_copy(1, M).start()
 
     far_pass(0, M)
-    far_y(M, start)
+    far_y(M)
     z_round(1, O)
     z_round(2, M)
 
@@ -325,7 +324,7 @@
                 @pl.when(far_wanted(side, who, kind, y))
                 def _():
                     spot = far.at[side, who, kind]
-                    remote(spot, spot, q_send.at[0], far_recv(side, who, kind), dev_c).wait_recv()
+                    remote(spot, spot, q_send, far_recv(side, who, kind), dev_c).wait_recv()
 
     def far_near(i, _):
         add(1, i // 5, (z + i % 5 + 6) % NZ)
@@ -389,17 +388,11 @@
     sent_all(left.at[pl.ds(0, NY)], c_send)
     sent_all(strip.at[0, O], f_send)
     sent_all(strip.at[0, O], local_sem.at[3])
-    far_y(M, lambda c: c.wait_send())
-    far_y(O, lambda c: c.wait_send())
-    for d in range(NY):
-        who = ((y + d) % NY) * NC + k
-        for kind in (M, O):
-            if (d, kind) != (0, O):
-                far_sends(d, kind, False)
-                for side in (0, 1):
-                    @pl.when(far_wanted(side, who, kind, y))
-                    def _():
-                        sent_all(far.at[side, who, kind], far_send(q_send, side, d, kind))
+    own_chunks = [(d, kind) for d in range(NY) for kind in (M, O) if (d, kind) != (0, O)]
+    wait_count([far_by_y(side, kind, there) for side in (0, 1) for kind in (M, O) for there in (y_up, y_dn)], fy_send)
+    wait_count([far_by_x(side, d, kind) for side in (0, 1) for d, kind in own_chunks], p_send)
+    wait_count([far_wanted(side, ((y + d) % NY) * NC + k, kind, y) for side in (0, 1) for d, kind in own_chunks],
+               q_send)
 
     for sent in range(NM):
         m = (sent + b_shift) % NM
@@ -441,9 +434,9 @@
             dma(()),
             dma(()),
             dma(()),
-            dma((9,)),
-            dma((9,)),
-            dma((2, 2)),
+            dma(()),
+            dma(()),
+            dma(()),
             dma(()),
             dma((4,)),
         ],

time: 74.8 us -> 74.6 us (level)
  no operation moved by 1% of the time
where the time goes in v8:
time: 74.6 us; the launch traced here: 74.5 us
  Pallas kernels  73.8 us (99%)
    pallas_call x1, Pallas kernels, exchange(): pl.pallas_call(kernel, out_shape=(pltpu.VMEM((NM, 2) + block, jnp.bfloat1...  73 us

profile of v8, /device:TPU:1, one launch (start us, length us, event | category | flops | bytes accessed | tf_op | source)
XLA Modules:
  0.0 74.5 jit_solution(11326539705055612934)
XLA Ops:
  0.6 73.0 %exchange.1 = (bf16[4,2,128,128]{3,2,1,0:T(8,128)(2,1)S(1)}, bf16[4,2,128,128]{3,2,1,0:T(8,128)(2,1)S(1)}) custom-call(bf16[4,2,128,128]{3,2,1,0:T(8,128)(2,1)} %bitcast.18, bf16[4,2,128,128]{3,2,1,0:T(8,128)(2,1)} %bitcast.19, bf16[4,2,128,128]{3,2,1,0:T(8,128)(2,1)} %bitcast.20, s32[2,4]{1,0:T(2,128)} %bitcast.21, s32[2,4]{1,0:T(2,128)} %bitcast.22, ...), custom_call_target="tpu_custom_call" | custom-call | tf_op jit(solution)/shard_map/exchange/pallas_call | solution.py:411
  73.7 0.8 %finish.1 = (bf16[4,2,128,128]{3,2,1,0:T(8,128)(2,1)}, bf16[4,2,128,128]{3,2,1,0:T(8,128)(2,1)}) custom-call(bf16[4,2,128,128]{3,2,1,0:T(8,128)(2,1)S(1)} %get-tuple-element.6.c_ref, bf16[4,2,128,128]{3,2,1,0:T(8,128)(2,1)S(1)} %get-tuple-element.7.r_ref), custom_call_target="tpu_custom_call" | custom-call | tf_op jit(solution)/shard_map/finish/pallas_call | solution.py:460

commit v9 on v8

--- a/solution.py
+++ b/solution.py
@@ -371,13 +371,23 @@
             put(m, M, c + acc[m, 0, 0], s + acc[m, 0, 1])
             r_copy(m).start()
         else:
-            total = []
-            for i in range(2):
-                for up in (True, False):
-                    z_part(up, i, 4).wait_recv()
-                out_f[m, i] = (one_product(1, m, opposite, 2 * i) + acc[m, 1, i]).astype(jnp.bfloat16)
-                total.append(one_product(0, m, opposite, 2 * i) + acc[m, 0, i])
-                r_part(i).start()
+            def half(r, i, j):
+                return jnp.dot(sides(r, m, opposite, (i,))[i],
+                               jnp.concatenate([strip[opposite, M, m, j], strip[opposite, O, m, j]], axis=0),
+                               preferred_element_type=jnp.float32)
+
+            for up in (True, False):
+                z_part(up, 0, 4).wait_recv()
+            out_f[m, 0] = (one_product(1, m, opposite, 0) + acc[m, 1, 0]).astype(jnp.bfloat16)
+            total = [one_product(0, m, opposite, 0) + acc[m, 0, 0]]
+            r_part(0).start()
+            for r in range(2):
+                acc[m, r, 1] += half(r, 2, 1)
+            for up in (True, False):
+                z_part(up, 1, 4).wait_recv()
+            out_f[m, 1] = (half(1, 1, 2) + acc[m, 1, 1]).astype(jnp.bfloat16)
+            total.append(half(0, 1, 2) + acc[m, 0, 1])
+            r_part(1).start()
             put(m, M, *total)
 
     def sent_all(ref, sem):

time: 74.6 us -> 74.6 us (level)
  no operation moved by 1% of the time
where the time goes in v9:
time: 74.6 us; the launch traced here: 74.5 us
  Pallas kernels  73.8 us (99%)
    pallas_call x1, Pallas kernels, exchange(): pl.pallas_call(kernel, out_shape=(pltpu.VMEM((NM, 2) + block, jnp.bfloat1...  73 us

profile of v9, /device:TPU:1, one launch (start us, length us, event | category | flops | bytes accessed | tf_op | source)
XLA Modules:
  0.0 74.5 jit_solution(18235073671804988389)
XLA Ops:
  0.6 73.0 %exchange.1 = (bf16[4,2,128,128]{3,2,1,0:T(8,128)(2,1)S(1)}, bf16[4,2,128,128]{3,2,1,0:T(8,128)(2,1)S(1)}) custom-call(bf16[4,2,128,128]{3,2,1,0:T(8,128)(2,1)} %bitcast.18, bf16[4,2,128,128]{3,2,1,0:T(8,128)(2,1)} %bitcast.19, bf16[4,2,128,128]{3,2,1,0:T(8,128)(2,1)} %bitcast.20, s32[2,4]{1,0:T(2,128)} %bitcast.21, s32[2,4]{1,0:T(2,128)} %bitcast.22, ...), custom_call_target="tpu_custom_call" | custom-call | tf_op jit(solution)/shard_map/exchange/pallas_call | solution.py:421
  73.7 0.8 %finish.1 = (bf16[4,2,128,128]{3,2,1,0:T(8,128)(2,1)}, bf16[4,2,128,128]{3,2,1,0:T(8,128)(2,1)}) custom-call(bf16[4,2,128,128]{3,2,1,0:T(8,128)(2,1)S(1)} %get-tuple-element.6.c_ref, bf16[4,2,128,128]{3,2,1,0:T(8,128)(2,1)S(1)} %get-tuple-element.7.r_ref), custom_call_target="tpu_custom_call" | custom-call | tf_op jit(solution)/shard_map/finish/pallas_call | solution.py:470
